TPU v7x, 768 devices: a whole 4x8x12 slice. The times are simulated.
768 devices in a mesh: kpt: 4 (over x), band: 16 (over y, core), plane: 12 (over z).
Axes of the slice: x: 4, y: 8, z: 12, core: 2. Of those that a mesh axis runs over, the one named last changes fastest.
Arguments:
- wavefunctions: float32 [4, 16, 2, 1920, 96], P('kpt', 'band', None, 'plane'), may hold values from -6 to 6
- resident: float32 [4, 256, 2, 1920, 96], P('kpt', 'band', None, 'plane'), may hold values from -0.078125 to 0.078125
- potential: float32 [96, 9216], P('plane'), may hold values from -5 to 5
- stick_column_table: int32 [4, 1920], P('kpt'), may hold values from 0 to 9216, as said below
- kpoint: float32 [4, 3], P('kpt'), may hold values from -0.5 to 0.5
Outputs:
- residual: float32 [4, 16, 2, 1920, 96], P('kpt', 'band', None, 'plane')
Inputs may be any that keep to these rules, and one draw needn't show every extreme that they name: `stick_column_table`: each row lists every column ix * 96 + iy whose signed frequencies satisfy mx^2 + my^2 <= 24^2 exactly once and no other column; every other slot holds 9216 and is empty. Slots p * 160 to (p + 1) * 160 - 1 are those of plane index p, and in every row the slots of some plane index are all live.
All inputs are finite; a program needn't handle non-finite values.
Results may differ from a plain program's by a relative error of at most 0.0003.
Values sent between devices are 32-bit elements; how exact they have to be, the bound alone decides.
A program may use at most 64 MiB of HBM per device.

v0:
```python
import math

import jax
import jax.numpy as jnp
from jax import lax
from jax.sharding import PartitionSpec as P

NG = 96


KINETIC = 12.0
HIGHEST = lax.Precision.HIGHEST


def complex_table(length, forward):
    positions = jnp.arange(length, dtype=jnp.int32)
    phases = positions[:, None] * positions[None, :] % length
    angles = phases.astype(jnp.float32) * (2.0 * math.pi / length)
    cosine = jnp.cos(angles)
    sine = jnp.sin(angles)
    if forward:
        from_real = jnp.stack([cosine, sine], axis=1)
        from_imag = jnp.stack([-sine, cosine], axis=1)
    else:
        from_real = jnp.stack([cosine, -sine], axis=1)
        from_imag = jnp.stack([sine, cosine], axis=1)
    return jnp.stack([from_real, from_imag])


def signed_index(values, length):
    return jnp.where(values < length // 2, values, values - length)


def contract_bands(form, left, right):
    return jnp.einsum(form, left, right, precision=HIGHEST, preferred_element_type=jnp.float32)


def paired_basis(basis_vectors):
    turned = jnp.stack([-basis_vectors[:, 1], basis_vectors[:, 0]], axis=1)
    return jnp.stack([basis_vectors, turned])


def margin_block(paired, fragment):
    return contract_bands("recsq,kcsq->rek", paired, fragment)


def correction_block(portion, paired):
    return contract_bands("reg,recsq->gcsq", portion, paired)


def on_device(wavefunctions, resident, potential, stick_column_table, kpoint):
    length = NG
    band_rows = wavefunctions.shape[1]
    slots = wavefunctions.shape[3]
    planes = potential.shape[0]
    table_plus = complex_table(length, True)
    table_minus = complex_table(length, False)
    all_columns = stick_column_table[0]
    local_columns = lax.dynamic_slice_in_dim(all_columns, lax.axis_index("plane") * slots, slots)
    live_local = (local_columns < length * length).astype(jnp.float32)
    live_mask = live_local[None, None, :, None]
    coeffs = wavefunctions[0] * live_mask
    stick_field = contract_bands("bcsq,cqrz->szbr", coeffs, table_plus)
    plane_sticks = lax.all_to_all(stick_field, "plane", split_axis=1, concat_axis=0, tiled=True)
    plane_grid = jnp.zeros((length * length, planes, band_rows, 2), jnp.float32)
    plane_grid = plane_grid.at[all_columns].set(plane_sticks, mode="drop")
    plane_grid = plane_grid.reshape(length, length, planes, band_rows, 2)
    rows_done = contract_bands("xqpbc,cqry->xypbr", plane_grid, table_plus)
    field = contract_bands("qypbc,cqrx->xypbr", rows_done, table_plus)
    weights = jnp.transpose(potential.reshape(planes, length, length), (1, 2, 0))
    product = field * weights[:, :, :, None, None]
    outer = contract_bands("xqpbc,cqry->xypbr", product, table_minus)
    spectrum = contract_bands("qypbc,cqrx->xypbr", outer, table_minus)
    spectrum = spectrum.reshape(length * length, planes, band_rows, 2)
    safe_columns = jnp.where(all_columns < length * length, all_columns, 0)
    picked = jnp.take(spectrum, safe_columns, axis=0)
    returned = lax.all_to_all(picked, "plane", split_axis=0, concat_axis=1, tiled=True)
    local_part = contract_bands("szbc,czrq->brsq", returned, table_minus)
    inverse_volume = 1.0 / length**3
    safe_local = jnp.where(local_columns < length * length, local_columns, 0)
    freq_x = signed_index(safe_local // length, length).astype(jnp.float32) + kpoint[0, 0]
    freq_y = signed_index(safe_local % length, length).astype(jnp.float32) + kpoint[0, 1]
    freq_z = (
        signed_index(jnp.arange(length, dtype=jnp.int32), length).astype(jnp.float32) + kpoint[0, 2]
    )
    kinetic = (
        KINETIC
        / (length * length)
        * ((freq_x * freq_x + freq_y * freq_y)[:, None] + (freq_z * freq_z)[None, :])
    )
    images = (local_part * inverse_volume + kinetic[None, None] * coeffs) * live_mask
    basis_vectors = resident[0] * live_mask
    paired = paired_basis(basis_vectors)
    block = margin_block(paired, lax.all_gather(images, "band", axis=0, tiled=True))
    margin = lax.psum(block, "plane")
    correction = lax.psum_scatter(
        correction_block(margin, paired), "band", scatter_dimension=0, tiled=True
    )
    residual = images - correction
    return residual[None]


def solution(mesh):
    in_specs = (
        P("kpt", "band", None, "plane", None),
        P("kpt", "band", None, "plane", None),
        P("plane", None),
        P("kpt", None),
        P("kpt", None),
    )
    out_specs = P("kpt", "band", None, "plane", None)
    return jax.shard_map(
        on_device, mesh=mesh, in_specs=in_specs, out_specs=out_specs, check_vma=False
    )
```

profile of v0, /device:TPU:1, one launch (start us, length us, event | category | flops | bytes accessed | tf_op | source)
XLA Modules:
  0.0 460.0 jit_solution(4798878303662636677)
XLA Ops:
  9.9 15.7 %all-to-all-start = ((f32[160,96,1,2]{0,3,2,1:T(2,128)}), f32[160,96,1,2]{0,3,2,1:T(2,128)S(1)}, u32[]{:S(2)}, u32[]{:S(2)}) async-start(f32[160,96,1,2]{0,3,2,1:T(2,128)} %copy.61), calls=%async_computation | async-start | bytes 393216 | tf_op jit(solution)/shard_map/all_to_all | solution.py:64
  31.0 7.1 %all-to-all-done = f32[160,96,1,2]{0,3,2,1:T(2,128)S(1)} async-done(((f32[160,96,1,2]{0,3,2,1:T(2,128)}), f32[160,96,1,2]{0,3,2,1:T(2,128)S(1)}, u32[]{:S(2)}, u32[]{:S(2)}) %all-to-all-start) | async-done | bytes 122912 | tf_op jit(solution)/shard_map/all_to_all | solution.py:64
  39.1 3.9 broadcast.324
  43.0 180.0 %scatter_fusion = f32[9216,8,2]{1,2,0:T(2,128)} fusion(f32[9216,8,2]{1,2,0:T(2,128)} %broadcast.324, s32[1920]{0:T(1024)S(1)} %get-tuple-element.6, f32[1920,8,2]{1,2,0:T(2,128)S(1)} %bitcast.171), kind=kCustom, calls=%fused_computation.1 | custom fusion | bytes 376320 | tf_op jit(solution)/shard_map/scatter | solution.py:66
  223.0 8.9 %copy.66 = f32[96,96,8,2]{1,0,3,2:T(8,128)S(1)} copy(f32[96,96,8,2]{2,3,1,0:T(2,128)} %bitcast.170) | data formatting | bytes 1179648 | tf_op jit(solution)/shard_map/reshape.8
  231.8 1.5 convolution_bitcast_fusion.3
  237.8 7.5 %copy.112 = f32[96,96,8,1,2]{2,4,1,0,3:T(2,128)} copy(f32[96,96,8,1,2]{1,0,2,4,3:T(8,128)S(1)} %convolution_bitcast_fusion.1) | data formatting | bytes 1179648 | tf_op jit(solution)/shard_map/reshape | solution.py:74
  245.3 7.8 %gather_fusion = f32[1920,8,2]{1,2,0:T(2,128)S(1)} fusion(f32[9216,8,2]{1,2,0:T(2,128)} %bitcast.172, s32[2048]{0:T(1024)S(1)} %pad_clamp_fusion), kind=kCustom, calls=%fused_computation | custom fusion | bytes 253440 | tf_op jit(solution)/shard_map/jit(_take)/gather | solution.py:76
  253.1 7.6 %fusion.56 = f32[1920,1,2,8]{3,2,1,0:T(2,128)} fusion(f32[1920,8,2]{1,2,0:T(2,128)S(1)} %gather_fusion, pred[1920]{0:T(1024)(128)(4,1)S(1)} %compare_and_fusion), kind=kLoop, calls=%fused_computation.97 | loop fusion | flops 30720 | bytes 247680
  260.7 5.3 %reshape.318 = f32[12,1,2560]{2,1,0:T(1,128)} reshape(f32[1920,1,2,8]{3,2,1,0:T(2,128)} %fusion.56) | data formatting | bytes 245760
  266.0 4.2 all-to-all-start.1
  271.1 9.6 %all-to-all-done.1 = f32[12,1,2560]{2,1,0:T(1,128)S(1)} async-done(((f32[12,1,2560]{2,1,0:T(1,128)}), f32[12,1,2560]{2,1,0:T(1,128)S(1)}, u32[]{:S(2)}, u32[]{:S(2)}) %all-to-all-start.1) | async-done | bytes 122912 | tf_op jit(solution)/shard_map/all_to_all | solution.py:77
  282.1 4.3 reshape.319
  286.4 2.8 copy.114
  290.5 1.5 bitcast_multiply_fusion
  292.4 1.6 copy-done.1
  293.9 3.1 copy_multiply_fusion
  297.0 35.6 %all-gather.2.cloned.1.call-done = f32[16,2,160,96]{3,2,1,0:T(8,128)} async-done(((f32[1,2,160,96]{3,2,1,0:T(8,128)}), f32[16,2,160,96]{3,2,1,0:T(8,128)}) %all-gather.2.cloned.1.call-update) | async-done | bytes 1966096 | tf_op jit(solution)/shard_map/all_gather | solution.py:94
  332.5 8.0 %fusion.11 = f32[2,16,16]{2,1,0:T(8,128)S(1)} fusion(f32[16,2,160,96,1]{3,2,1,0,4:T(8,128)} %bitcast.174, f32[1,16,2,160,96]{4,1,0,3,2:T(8,128)S(1)} %maximum_bitcast_fusion, f32[1,16,2,160,96]{4,1,0,3,2:T(8,128)} %copy_multiply_fusion), kind=kOutput, calls=%fused_computation.25 | convolution fusion | flops 189726720 | bytes 5900288 | tf_op jit(solution)/shard_map/recsq,kcsq->rek/dot_general | solution.py:35
  340.5 33.8 %psum.7 = f32[2,16,16]{2,1,0:T(8,128)S(1)} all-reduce(f32[2,16,16]{2,1,0:T(8,128)S(1)} %fusion.11), channel_id=1, replica_groups=mesh['kpt'=4,'band'=16,'plane'=12] {'plane'}, use_global_device_ids=true, to_apply=%region_1.2 | all-reduce | flops 512 | bytes 4096 | tf_op jit(solution)/shard_map/psum | solution.py:95
  374.3 4.7 %fusion.4 = f32[16,2,160,96]{3,0,2,1:T(8,128)S(1)} fusion(f32[1,16,2,160,96]{4,1,0,3,2:T(8,128)S(1)} %maximum_bitcast_fusion, f32[1,16,2,160,96]{4,1,0,3,2:T(8,128)} %copy_multiply_fusion, f32[2,16,16]{2,1,0:T(8,128)S(1)} %psum.7), kind=kOutput, calls=%fused_computation.11 | convolution fusion | flops 189726720 | bytes 5900288 | tf_op jit(solution)/shard_map/reg,recsq->gcsq/dot_general | solution.py:35
  379.0 2.3 copy.82
  381.3 70.2 %reduce-scatter.2.cloned.1.call-done = f32[1,2,160,96]{3,2,1,0:T(8,128)} async-done(((f32[16,2,160,96]{3,2,1,0:T(8,128)}), f32[1,2,160,96]{3,2,1,0:T(8,128)}) %reduce-scatter.2.cloned.1.call-update) | async-done | bytes 122896 | tf_op jit(solution)/shard_map/reduce_scatter | solution.py:96
  451.5 1.6 subtract_bitcast_fusion
  (37 shorter events, 18.0 us)
Async XLA Ops:
  9.9 28.1 %all-to-all-start = ((f32[160,96,1,2]{0,3,2,1:T(2,128)}), f32[160,96,1,2]{0,3,2,1:T(2,128)S(1)}, u32[]{:S(2)}, u32[]{:S(2)}) async-start(f32[160,96,1,2]{0,3,2,1:T(2,128)} %copy.61), calls=%async_computation | async-start | bytes 393216 | tf_op jit(solution)/shard_map/all_to_all | solution.py:64
  266.0 23.1 %copy-start.3 = (f32[1,1,2,160,96]{4,3,2,1,0:T(8,128)S(1)}, f32[1,1,2,160,96]{4,3,2,1,0:T(8,128)}, u32[]{:S(2)}) copy-start(f32[1,1,2,160,96]{4,3,2,1,0:T(8,128)} %param.5) | copy-start | bytes 368644
  266.0 14.6 %all-to-all-start.1 = ((f32[12,1,2560]{2,1,0:T(1,128)}), f32[12,1,2560]{2,1,0:T(1,128)S(1)}, u32[]{:S(2)}, u32[]{:S(2)}) async-start(f32[12,1,2560]{2,1,0:T(1,128)} %reshape.318), calls=%async_computation.1 | async-start | bytes 245760 | tf_op jit(solution)/shard_map/all_to_all | solution.py:77
  270.2 62.3 %all-gather.2.cloned.1.call-start = ((), (), s32[]{:S(2)}) async-start(), calls=%async_computation.3 | async-start | bytes 2785280 | tf_op jit(solution)/shard_map/all_gather | solution.py:94
  282.1 8.4 %copy-start = (f32[1,16,2,160,96]{4,3,2,1,0:T(8,128)S(1)}, f32[1,16,2,160,96]{4,3,2,1,0:T(8,128)}, u32[]{:S(2)}) copy-start(f32[1,16,2,160,96]{4,3,2,1,0:T(8,128)} %param.6) | copy-start | bytes 5898244
  290.4 161.1 %reduce-scatter.2.cloned.1.call-start = ((), (), s32[]{:S(2)}) async-start(), calls=%async_computation.4 | async-start | bytes 2785280 | tf_op jit(solution)/shard_map/reduce_scatter | solution.py:96
  292.2 1.7 copy-start.1
  381.3 70.2 %copy-start.2 = (f32[1,2,160,96]{3,2,1,0:T(8,128)S(1)}, f32[1,2,160,96]{3,2,1,0:T(8,128)}, u32[]{:S(2)}) copy-start(f32[1,2,160,96]{3,2,1,0:T(8,128)} %fusion.10) | copy-start | bytes 368644
Sparse Core Ops, SparseCore 0:
  290.5 41.9 all-gather.1
  381.4 70.0 reduce-scatter.1
where the time goes:
time: 463 us; the launch traced here: 460 us
  local copies, waits for them, and re-layouts  229 us (49%)
  waiting for transfers between devices  122 us (26%)
  blocking collectives  33.8 us (7%)
  matrix products  21.1 us (5%)
  starting transfers between devices  20 us (4%)
  other arithmetic  19.8 us (4%)
  between operations  13.6 us (3%)
    scatter x1, local copies, waits for them, and re-layouts, on_device(): plane_grid = plane_grid.at[all_columns].set(plane_sticks, mode='drop')  180 us
    reduce_scatter x1, waiting for transfers between devices, on_device(): lax.psum_scatter(correction_block(margin, paired), 'band', scatter_dimens...  70.2 us
    all_gather x1, waiting for transfers between devices, on_device(): lax.all_gather(images, 'band', axis=0, tiled=True)  35.6 us
    psum x1, blocking collectives, on_device(): margin = lax.psum(block, 'plane')  33.8 us
    dot_general x8, matrix products, contract_bands(): jnp.einsum(form, left, right, precision=HIGHEST, preferred_element_type=j...  21.1 us
    all_to_all x1, starting transfers between devices, on_device(): lax.all_to_all(stick_field, 'plane', split_axis=1, concat_axis=0, tiled=T...  15.7 us
    unnamed x10, local copies, waits for them, and re-layouts  11.2 us
    all_to_all x1, waiting for transfers between devices, on_device(): lax.all_to_all(picked, 'plane', split_axis=0, concat_axis=1, tiled=True)  9.61 us
  transfers between devices with their start and end apart: 4, of which 4 were waited for; matrix products, arithmetic and copies ran while one was open for 2% of the time, Pallas kernels for 0%

commit v1 on v0

v1 whole, which is shorter than its diff:
```python
import functools
import math

import jax
import jax.numpy as jnp
import numpy as np
from jax import lax
from jax.experimental import pallas as pl
from jax.experimental.pallas import tpu as pltpu
from jax.sharding import PartitionSpec as P

NG = 96
KINETIC = 12.0
HIGHEST = lax.Precision.HIGHEST
MESH = pl.DeviceIdType.MESH
RAD = NG // 4
IXP = 64
LP = 128
F32 = jnp.float32
BF16 = jnp.bfloat16


def split_np(table):
    table = np.asarray(table, np.float32)
    high = table.astype(jnp.bfloat16)
    low = (table - high.astype(np.float32)).astype(jnp.bfloat16)
    return high, low


def tables():
    turn = 2.0 * math.pi / NG
    grid = np.arange(NG)
    full = np.outer(grid, grid) % NG * turn
    tz = np.concatenate([np.cos(full), np.sin(full)], axis=0)
    signed = np.arange(IXP) - RAD
    inside = (np.arange(IXP) <= 2 * RAD).astype(np.float64)
    part = np.outer(grid, signed) % NG * turn
    cosine = np.cos(part) * inside
    sine = np.sin(part) * inside
    pad = np.zeros((LP - NG, IXP))
    cy = np.concatenate([cosine, pad])
    sy = np.concatenate([sine, pad])
    ty = np.concatenate([cy, sy, -sy, cy], axis=0)
    xf = np.block([[cosine, -sine], [sine, cosine]])
    xb = np.block([[cosine.T, sine.T], [-sine.T, cosine.T]]) / float(NG) ** 3
    zb = np.zeros((LP, 2 * LP))
    zb[:NG, :NG] = np.cos(full)
    zb[:NG, LP : LP + NG] = np.sin(full)
    return [part for table in (tz, ty, xf, xb, zb) for part in split_np(table)]


def split(value):
    high = value.astype(BF16)
    low = (value - high.astype(F32)).astype(BF16)
    return high, low


def dot3(left, right, axes):
    dims = (((axes[0],), (axes[1],)), ((), ()))

    def one(a, b):
        return lax.dot_general(a, b, dims, preferred_element_type=F32)

    return one(left[0], right[0]) + (one(left[1], right[0]) + one(left[0], right[1]))


def local_kernel(
    nz, slots, planes,
    wf_ref, table_ref, pot_ref, kp_ref,
    tzh, tzl, tyh, tyl, xfh, xfl, xbh, xbl, zbh, zbl,
    out_ref,
    send1, recv1, send2, recv2, bth, btl, lhh, lhl, mask, vall, pick, extra, trans, livecol,
    ssem1, rsem1, ssem2, rsem2,
    projector,
):
    me = lax.axis_index("plane")
    total = nz * slots
    barrier = pltpu.get_barrier_semaphore()
    for step in range(1, nz):
        pl.semaphore_signal(barrier, inc=1, device_id={"plane": lax.rem(me + step, nz)}, device_id_type=MESH)

    greeted = projector.greet(barrier)

    forward = (tzh[...], tzl[...])
    from_real = dot3(forward, split(wf_ref[0]), (1, 1))
    from_imag = dot3(forward, split(wf_ref[1]), (1, 1))
    real = from_real[:NG] - from_imag[NG:]
    imag = from_imag[:NG] + from_real[NG:]
    send1[:, :, 0:slots] = real.reshape(nz, planes, slots)
    send1[:, :, slots : 2 * slots] = imag.reshape(nz, planes, slots)
    send1[:, :, 2 * slots :] = jnp.zeros((nz, planes, send1.shape[2] - 2 * slots), F32)
    pl.semaphore_wait(barrier, nz - 1 + greeted)

    def exchange(source, target, ssem, rsem):
        copies = []
        for step in range(1, nz):
            there = lax.rem(me + step, nz)
            copies.append(
                pltpu.make_async_remote_copy(
                    src_ref=source.at[there],
                    dst_ref=target.at[me],
                    send_sem=ssem.at[step],
                    recv_sem=rsem.at[step],
                    device_id={"plane": there},
                    device_id_type=MESH,
                )
            )
        order = sorted(range(nz - 1), key=lambda i: -min(i + 1, nz - 1 - i))
        for i in order:
            copies[i].start()
        target[me] = source[me]
        return copies

    copies1 = exchange(send1, recv1, ssem1, rsem1)

    projector.start_resident()

    columns = table_ref[...].astype(F32)
    alive = columns < float(NG * NG)
    ix = ((columns + 0.5) * (1.0 / NG)).astype(jnp.int32).astype(F32)
    iy = columns - ix * NG
    mx = jnp.where(ix < NG // 2, ix, ix - NG)
    my = jnp.where(iy < NG // 2, iy, iy - NG)
    kx = jnp.where(alive, mx + RAD, -1.0)
    ky = jnp.where(alive, my + RAD, -1.0)
    rows = lax.broadcasted_iota(jnp.int32, (IXP, total), 0).astype(F32)
    hot_x = jnp.where(rows == kx, 1.0, 0.0)
    hot_y = jnp.where(rows == ky, 1.0, 0.0).astype(BF16)
    mask[:, 0:total] = hot_x
    mask[:, total:] = hot_x
    for c in range(2):
        for tab, into in ((tyh, bth), (tyl, btl)):
            into[:, c * total : (c + 1) * total] = jnp.dot(
                tab[c * 2 * LP : (c + 1) * 2 * LP, :], hot_y, preferred_element_type=F32
            ).astype(BF16)
    fx = mx + kp_ref[0, 0]
    fy = my + kp_ref[0, 1]
    sheet = fx * fx + fy * fy
    live = jnp.where(alive, 1.0, 0.0)
    for q in range(nz):
        extra[q, 0:1, 0:slots] = sheet[:, q * slots : (q + 1) * slots]
        extra[q, 1:2, 0:slots] = live[:, q * slots : (q + 1) * slots]

    for copy in copies1:
        copy.wait()
    for q in range(nz):
        vall[:, q * slots : (q + 1) * slots] = recv1[q, :, 0:slots]
        vall[:, total + q * slots : total + (q + 1) * slots] = recv1[q, :, slots : 2 * slots]

    wide = 256
    @pl.loop(0, 2 * total // wide)
    def _(chunk):
        lanes = pl.ds(pl.multiple_of(chunk * wide, wide), wide)
        hot = mask[:, lanes].astype(BF16)
        values = vall[:, lanes]
        for z in range(planes):
            row = jnp.broadcast_to(values[z : z + 1], (16, wide))
            high, low = split(row)
            for g in range(IXP // 16):
                part = hot[g * 16 : (g + 1) * 16]
                lhh[z * IXP + g * 16 : z * IXP + (g + 1) * 16, lanes] = part * high
                lhl[z * IXP + g * 16 : z * IXP + (g + 1) * 16, lanes] = part * low

    rows_done = dot3((lhh[...], lhl[...]), (bth[...], btl[...]), (1, 1))
    to_x = (xfh[...], xfl[...])
    to_k = (xbh[...], xbl[...])
    spectrum = []
    for z in range(0, planes, 2):
        a = rows_done[z * IXP : (z + 1) * IXP]
        b = rows_done[(z + 1) * IXP : (z + 2) * IXP]
        pair = jnp.concatenate(
            [jnp.concatenate([a[:, :LP], b[:, :LP]], 1), jnp.concatenate([a[:, LP:], b[:, LP:]], 1)], 0
        )
        field = dot3(to_x, split(pair), (1, 0))
        zeros = jnp.zeros((NG, LP - NG), F32)
        weight = jnp.concatenate([pot_ref[z], zeros, pot_ref[z + 1], zeros], 1)
        product = field * jnp.concatenate([weight, weight], 0)
        back = dot3(to_k, split(product), (1, 0))
        for h in range(2):
            spectrum.append(
                jnp.concatenate(
                    [back[:IXP, h * LP : (h + 1) * LP], back[IXP:, h * LP : (h + 1) * LP]], 1
                )
            )
    spread = split(jnp.concatenate(spectrum, 0))

    for chunk in range(2 * total // wide):
        lanes = slice(chunk * wide, (chunk + 1) * wide)
        found = dot3(spread, (bth[:, lanes], btl[:, lanes]), (1, 0))
        found = found.reshape(planes, IXP, wide) * mask[:, lanes][None]
        pick[:, lanes] = jnp.sum(found, axis=1)

    send2[:, :, 2 * slots :] = jnp.zeros((nz, planes, send2.shape[2] - 2 * slots), F32)
    for q in range(nz):
        send2[q, :, 0:slots] = pick[:, q * slots : (q + 1) * slots]
        send2[q, :, slots : 2 * slots] = pick[:, total + q * slots : total + (q + 1) * slots]
    copies2 = exchange(send2, recv2, ssem2, rsem2)
    trans[NG:, :] = jnp.zeros((LP - NG, trans.shape[1]), F32)
    trans[NG : NG + 2, 0:slots] = extra[me, 0:2, 0:slots]
    freq = lax.broadcasted_iota(jnp.int32, (1, NG), 1)
    fz = jnp.where(freq < NG // 2, freq, freq - NG).astype(F32) + kp_ref[0, 2]
    projector.finish_resident()
    projector.flatten_resident()
    for copy in copies2:
        copy.wait()
    trans[0:NG, :] = recv2[...].reshape(NG, trans.shape[1])
    turned = trans[...].T
    both = turned[: 2 * slots]
    result = dot3(split(both), (zbh[...], zbl[...]), (1, 0))
    alive = turned[:slots, NG + 1 : NG + 2]
    kinetic = (KINETIC / (NG * NG)) * (turned[:slots, NG : NG + 1] + fz * fz) * alive
    images = (
        (result[:slots, :LP] + result[slots:, LP:])[:, :NG] + kinetic * wf_ref[0],
        (result[slots:, :LP] - result[:slots, LP:])[:, :NG] + kinetic * wf_ref[1],
    )
    projector.pack(images)
    for c in range(2):
        out_ref[c] = images[c]
    livecol[...] = jnp.broadcast_to(alive, livecol.shape)
    projector.gather()
    margin = projector.margin()
    projector.correct(margin)
    projector.scatter()
    for c in range(2):
        out_ref[c] = out_ref[c] - livecol[...] * projector.correction(c)


ORDER = (0, 1, 7, 2, 6, 3, 5, 4)


class Projector:
    def __init__(self, nz, slots, rows, refs):
        (self.res, self.dbuf, self.dh, self.dl, self.packed, self.abuf, self.ih, self.il, self.mpair, self.mall,
         self.cbuf, self.rbuf, self.fbuf, self.unpacked,
         self.dsem, self.psem, self.agsem, self.mpsem, self.mssem, self.mrsem, self.rssem, self.fsem) = refs
        self.nz, self.half, self.rows = nz, slots // 2, rows
        self.lines = self.half * NG // LP
        self.block = 2 * self.lines
        band = lax.axis_index("band")
        nb = 16
        self.me = lax.axis_index("plane")
        self.core = lax.rem(band, 2)
        self.partner = {"band": band + 1 - 2 * self.core}
        self.right = {"band": lax.rem(band + 2, nb)}
        self.left = {"band": lax.rem(band + nb - 2, nb)}

    def remote(self, src, dst, send, recv, device):
        return pltpu.make_async_remote_copy(
            src_ref=src, dst_ref=dst, send_sem=send, recv_sem=recv, device_id=device, device_id_type=MESH
        )

    def greet(self, barrier):
        for device in (self.partner, self.right, self.left):
            pl.semaphore_signal(barrier, inc=1, device_id=device, device_id_type=MESH)
        return 3

    def slab(self, i):
        place = (self.core * self.rows * 2 + i) * self.half
        return self.dbuf.at[pl.ds(pl.multiple_of(place, 8), self.half), :]

    def local_fetch(self, i):
        own = pl.ds(pl.multiple_of(self.core * self.half, 8), self.half)
        return pltpu.make_async_copy(self.res.at[i, own, :], self.slab(i), self.dsem.at[0, i])

    def swap_resident(self, i):
        other = pl.ds(pl.multiple_of((1 - self.core) * self.half, 8), self.half)
        return self.remote(
            self.res.at[i, other, :], self.slab(i), self.dsem.at[1, i], self.dsem.at[2, i], self.partner
        )

    def start_resident(self):
        @pl.loop(0, 2 * self.rows)
        def _(i):
            self.swap_resident(i).start()
            self.local_fetch(i).start()

    def finish_resident(self):
        @pl.loop(0, 2 * self.rows)
        def _(i):
            self.swap_resident(i).wait()
            self.local_fetch(i).wait()

    def flatten_resident(self):
        third = self.lines // 3
        span = 2 * self.half

        @pl.loop(0, third)
        def _(i):
            for c in range(2):
                for group in range(2 * self.rows // 16):
                    base = group * 16 * span + c * self.half + i
                    tail = self.dbuf[pl.ds(base + self.lines, 16, stride=span), :]
                    for k in range(3):
                        head = self.dbuf[pl.ds(base + k * third, 16, stride=span), :]
                        line = jnp.concatenate([head, tail[:, k * 32 : (k + 1) * 32]], 1)
                        lanes = pl.ds(pl.multiple_of((k * third + i) * LP, LP), LP)
                        at = slice(c * 2 * self.rows + group * 16, c * 2 * self.rows + group * 16 + 16)
                        self.dh[at, lanes], self.dl[at, lanes] = split(line)

    def at(self, rel, sub):
        place = ORDER.index(rel % 8) * 2 + sub
        return pl.ds(pl.multiple_of(place * self.block, 8), self.block)

    def pack(self, images):
        third = self.lines // 3
        for hh in range(2):
            for c in range(2):
                part = images[c][hh * self.half : (hh + 1) * self.half]
                self.packed[hh, c * self.lines : (c + 1) * self.lines, 0:NG] = part[: self.lines, :NG]
                for k in range(3):
                    start = c * self.lines + k * third
                    self.packed[hh, start : start + third, NG:LP] = part[self.lines :, k * 32 : (k + 1) * 32]

    def gather(self):
        mine, other = self.core, 1 - self.core
        pair = self.remote(
            self.packed.at[other], self.abuf.at[self.at(0, mine)], self.psem.at[0], self.psem.at[1], self.partner
        )
        pair.start()
        self.abuf[self.at(0, mine), :] = self.packed[mine]

        def hop(way, step, sub):
            sign = -1 if way == 0 else 1
            return self.remote(
                self.abuf.at[self.at(sign * step, sub)],
                self.abuf.at[self.at(sign * (step + 1), sub)],
                self.agsem.at[0, way, step, sub],
                self.agsem.at[1, way, step, sub],
                self.right if way == 0 else self.left,
            )

        started = []
        for step in range(4):
            for turn, sub in enumerate((mine, other)):
                if step == 0 and turn == 1:
                    pair.wait()
                for way in range(2):
                    if step == 3:
                        if turn == 1:
                            continue
                        sub = way
                    if step > 0:
                        hop(way, step - 1, sub).wait_recv()
                    copy = hop(way, step, sub)
                    copy.start()
                    started.append(copy)
                    if step == 3:
                        hop(way, 2, 1 - way).wait_recv()
        self.started = started
        self.hop = hop

    def flatten_images(self):
        @pl.loop(0, self.lines)
        def _(r):
            lanes = pl.ds(pl.multiple_of(r * LP, LP), LP)
            for c in range(2):
                value = self.abuf[pl.ds(c * self.lines + r, 16, stride=self.block), :]
                self.ih[c * 16 : (c + 1) * 16, lanes], self.il[c * 16 : (c + 1) * 16, lanes] = split(value)

    def margin(self):
        for way in range(2):
            self.hop(way, 3, way).wait_recv()
        for copy in self.started:
            copy.wait_send()
        self.flatten_images()
        count = 2 * self.rows
        gram = dot3((self.ih[...], self.il[...]), (self.dh[...], self.dl[...]), (1, 1))
        real = gram[:16, :count] + gram[16:, count:]
        imag = gram[16:, :count] - gram[:16, count:]
        both = jnp.concatenate([real, imag], 1)
        self.mpair[0] = jnp.concatenate([both[:8], both[8:]], 1)
        swap = self.remote(self.mpair.at[0], self.mpair.at[1], self.mpsem.at[0], self.mpsem.at[1], self.partner)
        swap.start()
        swap.wait()
        self.mall[self.me] = self.mpair[0] + self.mpair[1]
        copies = []
        order = sorted(range(1, self.nz), key=lambda i: -min(i, self.nz - i))
        for step in order:
            there = lax.rem(self.me + step, self.nz)
            copy = self.remote(
                self.mall.at[self.me], self.mall.at[self.me],
                self.mssem.at[step], self.mrsem.at[step], {"plane": there},
            )
            copy.start()
            copies.append(copy)
        for copy in copies:
            copy.wait()
        flat = jnp.sum(self.mall[...], axis=0)
        both = jnp.concatenate([flat[:, : 2 * count], flat[:, 2 * count :]], 0)
        real, imag = both[:, :count], both[:, count:]
        return jnp.concatenate(
            [jnp.concatenate([real, -imag], 1), jnp.concatenate([imag, real], 1)], 0
        )

    def correct(self, margin):
        left = split(margin)
        batch = 4

        @pl.loop(0, self.lines // batch)
        def _(g):
            lanes = pl.ds(pl.multiple_of(g * batch * LP, LP), batch * LP)
            value = dot3(left, (self.dh[:, lanes], self.dl[:, lanes]), (1, 0))
            for i in range(batch):
                for c in range(2):
                    self.cbuf[pl.ds(c * self.lines + g * batch + i, 16, stride=self.block), :] = value[
                        c * 16 : (c + 1) * 16, i * LP : (i + 1) * LP
                    ]

    def scatter(self):
        def slot(way, k, sub):
            place = (way * 4 + k) * 2 + sub
            return pl.ds(place * self.block, self.block)

        def own(way, k, sub):
            return self.at(k if way == 0 else -k, sub)

        def hop(way, k, sub, source):
            return self.remote(
                source, self.rbuf.at[slot(way, k - 1, sub)],
                self.rssem.at[0, way, k - 1, sub], self.rssem.at[1, way, k - 1, sub],
                self.right if way == 0 else self.left,
            )

        sent = []
        for k in (4, 3, 2, 1, 0):
            for sub in range(2):
                for way in range(2):
                    first = 4 if sub == way else 3
                    if k > first:
                        continue
                    if k == first:
                        copy = hop(way, k, sub, self.cbuf.at[own(way, k, sub)])
                    else:
                        hop(way, k + 1, sub, self.cbuf.at[own(way, k + 1, sub)]).wait_recv()
                        if k == 0:
                            continue
                        here = slot(way, k, sub)
                        self.rbuf[here, :] = self.rbuf[here, :] + self.cbuf[own(way, k, sub), :]
                        copy = hop(way, k, sub, self.rbuf.at[here])
                    copy.start()
                    sent.append(copy)
        for sub in range(2):
            total = self.cbuf[self.at(0, sub), :] + self.rbuf[slot(0, 0, sub), :] + self.rbuf[slot(1, 0, sub), :]
            self.fbuf[sub] = total
        final = self.remote(
            self.fbuf.at[1 - self.core], self.fbuf.at[2], self.fsem.at[0], self.fsem.at[1], self.partner
        )
        final.start()
        for copy in sent:
            copy.wait_send()
        self.unpack(self.core, self.core)
        final.wait()
        self.unpack(2, 1 - self.core)

    def unpack(self, source, hh):
        third = self.lines // 3
        for c in range(2):
            start = c * self.lines
            self.unpacked[hh, c, 0 : self.lines, :] = self.fbuf[source, start : start + self.lines, 0:NG]
            for k in range(3):
                self.unpacked[hh, c, self.lines : self.half, k * 32 : (k + 1) * 32] = self.fbuf[
                    source, start + k * third : start + (k + 1) * third, NG:LP
                ]

    def correction(self, c):
        return jnp.concatenate([self.unpacked[0, c], self.unpacked[1, c]], 0)

    @staticmethod
    def scratch(nz, slots, rows):
        half = slots // 2
        lines = half * NG // LP
        block = 2 * lines
        dma = pltpu.SemaphoreType.DMA
        return [
            pltpu.VMEM((4 * rows * half, NG), F32),
            pltpu.VMEM((4 * rows, lines * LP), BF16),
            pltpu.VMEM((4 * rows, lines * LP), BF16),
            pltpu.VMEM((2, block, LP), F32),
            pltpu.VMEM((16 * block, LP), F32),
            pltpu.VMEM((32, lines * LP), BF16),
            pltpu.VMEM((32, lines * LP), BF16),
            pltpu.VMEM((2, 8, LP), F32),
            pltpu.VMEM((nz, 8, LP), F32),
            pltpu.VMEM((16 * block, LP), F32),
            pltpu.VMEM((16 * block, LP), F32),
            pltpu.VMEM((3, block, LP), F32),
            pltpu.VMEM((2, 2, half, NG), F32),
            dma((3, 2 * rows)), dma((2,)), dma((2, 2, 4, 2)), dma((2,)), dma((nz,)), dma((nz,)), dma((2, 2, 4, 2)), dma((2,)),
        ]


def kernel(nz, slots, planes, rows, *refs):
    inputs, rest = refs[:14], refs[14:]
    resident, out_ref = rest[0], rest[1]
    count = 18
    local_scratch, project_scratch = rest[2 : 2 + count], rest[2 + count :]
    projector = Projector(nz, slots, rows, (resident,) + project_scratch)
    local_kernel(nz, slots, planes, *inputs, out_ref, *local_scratch, projector=projector)


def on_device(wavefunctions, resident, potential, stick_column_table, kpoint, nz):
    slots = wavefunctions.shape[3]
    planes = potential.shape[0]
    rows = resident.shape[1]
    total = nz * slots
    lanes = -(-2 * slots // LP) * LP
    vmem = pl.BlockSpec(memory_space=pltpu.VMEM)
    consts = [jnp.asarray(t) for t in tables()]
    block = pltpu.VMEM((nz, planes, lanes), F32)
    dma = pltpu.SemaphoreType.DMA
    out = pl.pallas_call(
        functools.partial(kernel, nz, slots, planes, rows),
        out_shape=jax.ShapeDtypeStruct((2, slots, NG), F32),
        in_specs=[vmem, vmem, vmem, pl.BlockSpec(memory_space=pltpu.SMEM)]
        + [vmem] * len(consts)
        + [pl.BlockSpec(memory_space=pl.ANY)],
        out_specs=vmem,
        scratch_shapes=[
            block, block, block, block,
            pltpu.VMEM((2 * LP, 2 * total), BF16),
            pltpu.VMEM((2 * LP, 2 * total), BF16),
            pltpu.VMEM((planes * IXP, 2 * total), BF16),
            pltpu.VMEM((planes * IXP, 2 * total), BF16),
            pltpu.VMEM((IXP, 2 * total), F32),
            pltpu.VMEM((planes, 2 * total), F32),
            pltpu.VMEM((planes, 2 * total), F32),
            pltpu.VMEM((nz, 8, lanes), F32),
            pltpu.VMEM((LP, lanes), F32),
            pltpu.VMEM((slots, NG), F32),
            dma((nz,)), dma((nz,)), dma((nz,)), dma((nz,)),
        ]
        + Projector.scratch(nz, slots, rows),
        compiler_params=pltpu.CompilerParams(collective_id=0, has_side_effects=True),
    )(
        wavefunctions[0, 0], stick_column_table, potential.reshape(planes, NG, NG), kpoint, *consts,
        resident[0].reshape(2 * rows, slots, NG),
    )
    return out[None, None]


def solution(mesh):
    in_specs = (
        P("kpt", "band", None, "plane", None),
        P("kpt", "band", None, "plane", None),
        P("plane", None),
        P("kpt", None),
        P("kpt", None),
    )
    out_specs = P("kpt", "band", None, "plane", None)
    return jax.shard_map(
        functools.partial(on_device, nz=mesh.shape["plane"]),
        mesh=mesh, in_specs=in_specs, out_specs=out_specs, check_vma=False,
    )
```

time: 463 us -> 101 us (0.22)
  local copies, waits for them, and re-layouts: 229 us -> 3.45 us
  waiting for transfers between devices: 122 us -> 0 us
  Pallas kernels: 0 us -> 97.2 us
  blocking collectives: 33.8 us -> 0 us
  matrix products: 21.1 us -> 0 us
  starting transfers between devices: 20 us -> 0 us
  other arithmetic: 19.8 us -> 0 us
  between operations: 13.6 us -> 0.01 us
    scatter x1 -> x0, local copies, waits for them, and re-layouts: 180 us -> none  [on_device(): plane_grid = plane_grid.at[all_columns].set(plane_sticks, mode='drop')]
    pallas_call x0 -> x1, Pallas kernels: none -> 97.2 us  [on_device(): pl.pallas_call(functools.partial(kernel, nz, slots, planes, rows), out_sh...]
    reduce_scatter x1 -> x0, waiting for transfers between devices: 70.2 us -> none  [on_device(): lax.psum_scatter(correction_block(margin, paired), 'band', scatter_dimens...]
    all_gather x1 -> x0, waiting for transfers between devices: 35.6 us -> none  [on_device(): lax.all_gather(images, 'band', axis=0, tiled=True)]
    psum x1 -> x0, blocking collectives: 33.8 us -> none  [on_device(): margin = lax.psum(block, 'plane')]
    dot_general x8 -> x0, matrix products: 21.1 us -> none  [contract_bands(): jnp.einsum(form, left, right, precision=HIGHEST, preferred_element_type=j...]
    all_to_all x2 -> x0, starting transfers between devices: 19.9 us -> none  [the longest x1 15.7 us: on_device(): lax.all_to_all(stick_field, 'plane', split_axis=1, concat_axis=0, tiled=T...]
    all_to_all x2 -> x0, waiting for transfers between devices: 16.7 us -> none  [the longest x1 9.61 us: on_device(): lax.all_to_all(picked, 'plane', split_axis=0, concat_axis=1, tiled=True)]
  transfers between devices with their start and end apart: 4 -> 0, of which waited for: 4 -> 0; matrix products, arithmetic and copies ran while one was open for 2% -> 0% of each run, Pallas kernels for 0% -> 0%
where the time goes in v1:
time: 101 us
  Pallas kernels  97.2 us (96%)
  local copies, waits for them, and re-layouts  3.45 us (3%)
    pallas_call x1, Pallas kernels, on_device(): pl.pallas_call(functools.partial(kernel, nz, slots, planes, rows), out_sh...  97.2 us

profile of v1, /device:TPU:1, one launch (start us, length us, event | category | flops | bytes accessed | tf_op | source)
XLA Modules:
  0.0 100.7 jit_solution(8605226926209213374)
XLA Ops:
  0.0 1.9 %reshape.3.refs_2_ = f32[8,96,96]{2,1,0:T(8,128)} reshape(f32[8,9216]{1,0:T(8,128)} %param.17) | data formatting | bytes 589824 | tf_op jit(solution)/shard_map/reshape | solution.py:535
  1.9 97.2 %shard_map.145 = f32[2,160,96]{2,1,0:T(8,128)} custom-call(f32[2,160,96]{2,1,0:T(8,128)} %bitcast.5, s32[1,1920]{1,0:T(1,128)} %refs_1_.1, f32[8,96,96]{2,1,0:T(8,128)} %reshape.3.refs_2_, f32[1,3]{1,0:T(1,128)} %refs_3_.1, bf16[192,96]{1,0:T(8,128)(2,1)} %constant.20.clone.refs_4_, bf16[192,96]{1,0:T(8,128)(2,1)} %constant.21.clone.refs_5_, ...), custom_call_target="tpu_custom_call" | custom-call | tf_op jit(solution)/shard_map/pallas_call | solution.py:511
  99.1 1.6 %copy.17 = f32[1,1,2,160,96]{4,3,2,1,0:T(8,128)} copy(f32[1,1,2,160,96]{4,3,2,1,0:T(8,128)} %bitcast.4) | data formatting | bytes 245760

commit v2 on v1

v2 whole, which is shorter than its diff:
```python
import functools
import math

import jax
import jax.numpy as jnp
import numpy as np
from jax import lax
from jax.experimental import pallas as pl
from jax.experimental.pallas import tpu as pltpu
from jax.sharding import PartitionSpec as P

NG = 96
KINETIC = 12.0
HIGHEST = lax.Precision.HIGHEST
MESH = pl.DeviceIdType.MESH
RAD = NG // 4
IXP = 64
LP = 128
F32 = jnp.float32
BF16 = jnp.bfloat16


def split_np(table):
    table = np.asarray(table, np.float32)
    high = table.astype(jnp.bfloat16)
    low = (table - high.astype(np.float32)).astype(jnp.bfloat16)
    return high, low


def tables():
    turn = 2.0 * math.pi / NG
    grid = np.arange(NG)
    full = np.outer(grid, grid) % NG * turn
    tz = np.concatenate([np.cos(full), np.sin(full)], axis=0)
    signed = np.arange(IXP) - RAD
    inside = (np.arange(IXP) <= 2 * RAD).astype(np.float64)
    part = np.outer(grid, signed) % NG * turn
    cosine = np.cos(part) * inside
    sine = np.sin(part) * inside
    pad = np.zeros((LP - NG, IXP))
    cy = np.concatenate([cosine, pad])
    sy = np.concatenate([sine, pad])
    ty = np.block([[cy, -sy], [sy, cy]])
    xf = np.block([[cosine, -sine], [sine, cosine]])
    xb = np.block([[cosine.T, sine.T], [-sine.T, cosine.T]]) / float(NG) ** 3
    zb = np.zeros((LP, 2 * LP))
    zb[:NG, :NG] = np.cos(full)
    zb[:NG, LP : LP + NG] = np.sin(full)
    return [np.stack(split_np(table)) for table in (tz, ty, xf, xb, zb)]


def split(value):
    high = value.astype(BF16)
    low = (value - high.astype(F32)).astype(BF16)
    return high, low


def dot3(left, right, axes):
    dims = (((axes[0],), (axes[1],)), ((), ()))

    def one(a, b):
        return lax.dot_general(a, b, dims, preferred_element_type=F32)

    return one(left[0], right[0]) + (one(left[1], right[0]) + one(left[0], right[1]))


def local_kernel(
    nz, slots, planes,
    inputs, out_ref,
    wf_ref, table_ref, pot_ref, kp_ref, tz, ty, xf, xb, zb, insem,
    send1, recv1, send2, recv2, bth, btl, lhh, lhl, mask, acc, sph, spl, tabx, weights, trans, livecol,
    ssem1, rsem1, ssem2, rsem2,
    projector,
):
    me = lax.axis_index("plane")
    lanes = send1.shape[2]
    barrier = pltpu.get_barrier_semaphore()
    for step in range(1, nz):
        pl.semaphore_signal(barrier, inc=1, device_id={"plane": lax.rem(me + step, nz)}, device_id_type=MESH)
    greeted = projector.greet(barrier)
    held = (wf_ref, table_ref, pot_ref, kp_ref, tz, ty, xf, xb, zb)
    fetches = [pltpu.make_async_copy(a, b, insem.at[i]) for i, (a, b) in enumerate(zip(inputs, held))]
    for i in (0, 4, 1, 5, 2, 3, 6, 7, 8):
        fetches[i].start()
    fetches[0].wait()
    fetches[4].wait()

    forward = (tz[0], tz[1])
    from_real = dot3(forward, split(wf_ref[0]), (1, 1))
    from_imag = dot3(forward, split(wf_ref[1]), (1, 1))
    real = from_real[:NG] - from_imag[NG:]
    imag = from_imag[:NG] + from_real[NG:]
    send1[:, :, 0:slots] = real.reshape(nz, planes, slots)
    send1[:, :, slots : 2 * slots] = imag.reshape(nz, planes, slots)
    send1[:, :, 2 * slots :] = jnp.zeros((nz, planes, lanes - 2 * slots), F32)
    pl.semaphore_wait(barrier, nz - 1 + greeted)

    def transfer(source, target, ssem, rsem, step):
        there = lax.rem(me + step, nz)
        return pltpu.make_async_remote_copy(
            src_ref=source.at[there],
            dst_ref=target.at[me],
            send_sem=ssem.at[step],
            recv_sem=rsem.at[step],
            device_id={"plane": there},
            device_id_type=MESH,
        )

    out1 = [transfer(send1, recv1, ssem1, rsem1, step) for step in range(1, nz)]
    for step in sorted(range(1, nz), key=lambda i: -min(i, nz - i)):
        out1[step - 1].start()
    projector.start_resident()
    for i in (1, 5, 2, 3, 6, 7, 8):
        fetches[i].wait()

    tabx[...] = jnp.full(tabx.shape, float(NG * NG), F32)
    columns = table_ref[...].astype(F32)
    for q in range(nz):
        part = columns[:, q * slots : (q + 1) * slots]
        tabx[q : q + 1, 0:slots] = part
        tabx[q : q + 1, slots : 2 * slots] = part

    def decode(column):
        ix = ((column + 0.5) * (1.0 / NG)).astype(jnp.int32).astype(F32)
        iy = column - ix * NG
        return jnp.where(ix < NG // 2, ix, ix - NG), jnp.where(iy < NG // 2, iy, iy - NG)

    def block_lanes(q):
        return pl.ds(pl.multiple_of(q * lanes, LP), lanes)

    second = lax.broadcasted_iota(jnp.int32, (1, lanes), 1) >= slots
    rows = lax.broadcasted_iota(jnp.int32, (2 * IXP, lanes), 0).astype(F32)

    @pl.loop(0, nz)
    def _(q):
        column = tabx[pl.ds(q, 1), :]
        alive = column < float(NG * NG)
        mx, my = decode(column)
        kx = jnp.where(alive, mx + RAD, -1.0)
        ky = jnp.where(alive, my + RAD + jnp.where(second, float(IXP), 0.0), -1.0)
        mask[:, block_lanes(q)] = jnp.where(rows[:IXP] == kx, 1.0, 0.0)
        hot = jnp.where(rows == ky, 1.0, 0.0).astype(BF16)
        for i, into in ((0, bth), (1, btl)):
            into[:, block_lanes(q)] = jnp.dot(ty[i], hot, preferred_element_type=F32).astype(BF16)

    zeros = jnp.zeros((weights.shape[0], LP - NG), F32)
    weights[:, NG:LP] = zeros
    for x in range(NG):
        weights[pl.ds(x, planes, stride=NG), 0:NG] = pot_ref[:, x * NG : (x + 1) * NG]

    for pair in range(nz // 2):
        offsets = ((nz - pair) % nz, pair + 1)
        owners = [lax.rem(me + offset, nz) for offset in offsets]
        side = pair % 2
        for place, (offset, q) in enumerate(zip(offsets, owners)):
            if offset == 0:
                values = send1[me]
            else:
                out1[(nz - offset) - 1].wait_recv()
                values = recv1[q]
            hot = mask[:, block_lanes(q)].astype(BF16)
            into = slice(place * lanes, (place + 1) * lanes)
            for z in range(planes):
                high, low = split(jnp.broadcast_to(values[z : z + 1], (16, lanes)))
                for g in range(IXP // 16):
                    part = hot[g * 16 : (g + 1) * 16]
                    at = slice(z * IXP + g * 16, z * IXP + (g + 1) * 16)
                    lhh[side, at, into] = part * high
                    lhl[side, at, into] = part * low
        phase = tuple(jnp.concatenate([b[:, block_lanes(q)] for q in owners], 1) for b in (bth, btl))
        term = dot3((lhh[side], lhl[side]), phase, (1, 1))
        acc[...] = term if pair == 0 else acc[...] + term

    to_x = (xf[0], xf[1])
    to_k = (xb[0], xb[1])
    for z in range(0, planes, 2):
        a = acc[z * IXP : (z + 1) * IXP]
        b = acc[(z + 1) * IXP : (z + 2) * IXP]
        joined = jnp.concatenate(
            [jnp.concatenate([a[:, :LP], b[:, :LP]], 1), jnp.concatenate([a[:, LP:], b[:, LP:]], 1)], 0
        )
        field = dot3(to_x, split(joined), (1, 0))
        weight = jnp.concatenate([weights[z * NG : (z + 1) * NG], weights[(z + 1) * NG : (z + 2) * NG]], 1)
        product = field * jnp.concatenate([weight, weight], 0)
        back = dot3(to_k, split(product), (1, 0))
        for h in range(2):
            high, low = split(
                jnp.concatenate([back[:IXP, h * LP : (h + 1) * LP], back[IXP:, h * LP : (h + 1) * LP]], 1)
            )
            at = slice((z + h) * IXP, (z + h + 1) * IXP)
            sph[at], spl[at] = high, low

    out2 = []
    for pair in reversed(range(nz // 2)):
        offsets = ((nz - pair) % nz, pair + 1)
        owners = [lax.rem(me + offset, nz) for offset in offsets]
        phase = tuple(jnp.concatenate([b[:, block_lanes(q)] for q in owners], 1) for b in (bth, btl))
        hot = jnp.concatenate([mask[:, block_lanes(q)] for q in owners], 1)
        found = dot3((sph[...], spl[...]), phase, (1, 0))
        picked = jnp.sum(found.reshape(planes, IXP, 2 * lanes) * hot[None], axis=1)
        for place, (offset, q) in enumerate(zip(offsets, owners)):
            part = picked[:, place * lanes : (place + 1) * lanes]
            if offset == 0:
                recv2[me] = part
            else:
                send2[q] = part
                copy = transfer(send2, recv2, ssem2, rsem2, offset)
                copy.start()
                out2.append(copy)

    column = tabx[pl.ds(me, 1), :]
    mx, my = decode(column)
    fx = mx + kp_ref[0:1, 0:1]
    fy = my + kp_ref[0:1, 1:2]
    trans[NG:, :] = jnp.zeros((LP - NG, lanes), F32)
    trans[NG : NG + 1, :] = fx * fx + fy * fy
    trans[NG + 1 : NG + 2, :] = jnp.where(column < float(NG * NG), 1.0, 0.0)
    freq = lax.broadcasted_iota(jnp.int32, (1, NG), 1)
    fz = jnp.where(freq < NG // 2, freq, freq - NG).astype(F32) + kp_ref[0:1, 2:3]
    projector.finish_resident()
    projector.flatten_resident()
    for copy in out1:
        copy.wait_send()
    for copy in out2:
        copy.wait()
    trans[0:NG, :] = recv2[...].reshape(NG, lanes)
    turned = trans[...].T
    result = dot3(split(turned[: 2 * slots]), (zb[0], zb[1]), (1, 0))
    alive = turned[:slots, NG + 1 : NG + 2]
    kinetic = (KINETIC / (NG * NG)) * (turned[:slots, NG : NG + 1] + fz * fz) * alive
    images = (
        (result[:slots, :LP] + result[slots:, LP:])[:, :NG] + kinetic * wf_ref[0],
        (result[slots:, :LP] - result[:slots, LP:])[:, :NG] + kinetic * wf_ref[1],
    )
    projector.pack(images)
    for c in range(2):
        out_ref[c] = images[c]
    livecol[...] = jnp.broadcast_to(alive, livecol.shape)
    first_gram = projector.gather()
    projector.correct(projector.margin(first_gram))
    projector.scatter()
    for c in range(2):
        out_ref[c] = out_ref[c] - livecol[...] * projector.correction(c)


ORDER = (0, 1, 7, 2, 6, 3, 5, 4)


class Projector:
    def __init__(self, nz, slots, rows, refs):
        (self.res, self.dbuf, self.dh, self.dl, self.packed, self.abuf, self.ih, self.il, self.mpair, self.mall,
         self.cbuf, self.rbuf, self.fbuf, self.unpacked,
         self.dsem, self.psem, self.agsem, self.mpsem, self.mssem, self.mrsem, self.rssem, self.fsem) = refs
        self.nz, self.half, self.rows = nz, slots // 2, rows
        self.lines = self.half * NG // LP
        self.block = 2 * self.lines
        self.parts = ((0, 64), (64, self.block - 64))
        band = lax.axis_index("band")
        nb = 16
        self.me = lax.axis_index("plane")
        self.core = lax.rem(band, 2)
        self.partner = {"band": band + 1 - 2 * self.core}
        chip = band - self.core
        self.sides = (lax.rem(chip + 2, nb), lax.rem(chip + nb - 2, nb))

    def beside(self, way, core):
        return {"band": self.sides[way] + core}

    def remote(self, src, dst, send, recv, device):
        return pltpu.make_async_remote_copy(
            src_ref=src, dst_ref=dst, send_sem=send, recv_sem=recv, device_id=device, device_id_type=MESH
        )

    def greet(self, barrier):
        others = [self.beside(way, core) for way in range(2) for core in range(2)]
        for device in [self.partner] + others:
            pl.semaphore_signal(barrier, inc=1, device_id=device, device_id_type=MESH)
        return 5

    def slab(self, i):
        place = (self.core * self.rows * 2 + i) * self.half
        return self.dbuf.at[pl.ds(pl.multiple_of(place, 8), self.half), :]

    def local_fetch(self, i):
        own = pl.ds(pl.multiple_of(self.core * self.half, 8), self.half)
        return pltpu.make_async_copy(self.res.at[i, own, :], self.slab(i), self.dsem.at[0, i])

    def swap_resident(self, i):
        other = pl.ds(pl.multiple_of((1 - self.core) * self.half, 8), self.half)
        return self.remote(
            self.res.at[i, other, :], self.slab(i), self.dsem.at[1, i], self.dsem.at[2, i], self.partner
        )

    def start_resident(self):
        @pl.loop(0, 2 * self.rows)
        def _(i):
            self.swap_resident(i).start()
            self.local_fetch(i).start()

    def finish_resident(self):
        @pl.loop(0, 2 * self.rows)
        def _(i):
            self.swap_resident(i).wait()
            self.local_fetch(i).wait()

    def flatten_resident(self):
        third = self.lines // 3
        span = 2 * self.half

        @pl.loop(0, third)
        def _(i):
            for c in range(2):
                for group in range(2 * self.rows // 16):
                    base = group * 16 * span + c * self.half + i
                    tail = self.dbuf[pl.ds(base + self.lines, 16, stride=span), :]
                    for k in range(3):
                        head = self.dbuf[pl.ds(base + k * third, 16, stride=span), :]
                        line = jnp.concatenate([head, tail[:, k * 32 : (k + 1) * 32]], 1)
                        lanes = pl.ds(pl.multiple_of((k * third + i) * LP, LP), LP)
                        at = slice(c * 2 * self.rows + group * 16, c * 2 * self.rows + group * 16 + 16)
                        self.dh[at, lanes], self.dl[at, lanes] = split(line)

    def at(self, rel, sub, part=None):
        place = (ORDER.index(rel % 8) * 2 + sub) * self.block
        if part is None:
            return pl.ds(pl.multiple_of(place, 8), self.block)
        start, size = self.parts[part]
        return pl.ds(pl.multiple_of(place + start, 8), size)

    def pack(self, images):
        third = self.lines // 3
        for hh in range(2):
            for c in range(2):
                part = images[c][hh * self.half : (hh + 1) * self.half]
                self.packed[hh, c * self.lines : (c + 1) * self.lines, 0:NG] = part[: self.lines, :NG]
                for k in range(3):
                    start = c * self.lines + k * third
                    self.packed[hh, start : start + third, NG:LP] = part[self.lines :, k * 32 : (k + 1) * 32]

    def gather(self):
        mine, other = self.core, 1 - self.core
        pair = self.remote(
            self.packed.at[other], self.abuf.at[self.at(0, mine)], self.psem.at[0], self.psem.at[1], self.partner
        )
        sign = (-1, 1)

        def first(way, core, part):
            start, size = self.parts[part]
            return self.remote(
                self.packed.at[core, pl.ds(start, size)], self.abuf.at[self.at(sign[way], mine, part)],
                self.agsem.at[0, way, 0, core, part], self.agsem.at[1, way, 0, mine, part], self.beside(way, core),
            )

        def hop(way, step, sub, part):
            return self.remote(
                self.abuf.at[self.at(sign[way] * step, sub, part)],
                self.abuf.at[self.at(sign[way] * (step + 1), sub, part)],
                self.agsem.at[0, way, step, sub, part], self.agsem.at[1, way, step, sub, part],
                self.beside(way, mine),
            )

        started = [first(way, core, part) for part in range(2) for core in range(2) for way in range(2)]
        for copy in started:
            copy.start()
        pair.start()
        self.abuf[self.at(0, mine), :] = self.packed[mine]
        for step in (1, 2, 3):
            if step == 3:
                pair.wait()
                self.flatten_images(0)
            for part in range(2):
                for sub in range(2):
                    for way in range(2):
                        if step == 3 and sub != way:
                            continue
                        hop(way, step - 1, sub, part).wait_recv()
                        copy = hop(way, step, sub, part)
                        copy.start()
                        started.append(copy)
        first_gram = self.gram(0)
        for part in range(2):
            for way in range(2):
                hop(way, 2, 1 - way, part).wait_recv()
                hop(way, 3, way, part).wait_recv()
        for copy in started:
            copy.wait_send()
        return first_gram

    def flatten_images(self, group):
        @pl.loop(0, self.lines)
        def _(r):
            lanes = pl.ds(pl.multiple_of(r * LP, LP), LP)
            value = jnp.concatenate(
                [
                    self.abuf[pl.ds(group * 8 * self.block + c * self.lines + r, 8, stride=self.block), :]
                    for c in range(2)
                ],
                0,
            )
            self.ih[group, :, lanes], self.il[group, :, lanes] = split(value)

    def gram(self, group):
        count = 2 * self.rows
        gram = dot3((self.ih[group], self.il[group]), (self.dh[...], self.dl[...]), (1, 1))
        real = gram[:8, :count] + gram[8:, count:]
        imag = gram[8:, :count] - gram[:8, count:]
        return jnp.concatenate([real, imag], 1)

    def margin(self, first_gram):
        self.flatten_images(1)
        count = 2 * self.rows
        self.mpair[0] = jnp.concatenate([first_gram, self.gram(1)], 1)
        swap = self.remote(self.mpair.at[0], self.mpair.at[1], self.mpsem.at[0], self.mpsem.at[1], self.partner)
        swap.start()
        swap.wait()
        self.mall[self.me] = self.mpair[0] + self.mpair[1]
        copies = []
        for step in sorted(range(1, self.nz), key=lambda i: -min(i, self.nz - i)):
            copy = self.remote(
                self.mall.at[self.me], self.mall.at[self.me],
                self.mssem.at[step], self.mrsem.at[step], {"plane": lax.rem(self.me + step, self.nz)},
            )
            copy.start()
            copies.append(copy)
        for copy in copies:
            copy.wait()
        flat = jnp.sum(self.mall[...], axis=0)
        both = jnp.concatenate([flat[:, : 2 * count], flat[:, 2 * count :]], 0)
        real, imag = both[:, :count], both[:, count:]
        return jnp.concatenate(
            [jnp.concatenate([real, -imag], 1), jnp.concatenate([imag, real], 1)], 0
        )

    def correct(self, margin):
        left = split(margin)
        batch = 4

        @pl.loop(0, self.lines // batch)
        def _(g):
            lanes = pl.ds(pl.multiple_of(g * batch * LP, LP), batch * LP)
            value = dot3(left, (self.dh[:, lanes], self.dl[:, lanes]), (1, 0))
            for i in range(batch):
                for c in range(2):
                    self.cbuf[pl.ds(c * self.lines + g * batch + i, 16, stride=self.block), :] = value[
                        c * 16 : (c + 1) * 16, i * LP : (i + 1) * LP
                    ]

    def scatter(self):
        mine, other = self.core, 1 - self.core

        def slot(way, k, sub, part=None):
            place = ((way * 4 + k) * 2 + sub) * self.block
            start, size = (0, self.block) if part is None else self.parts[part]
            return pl.ds(pl.multiple_of(place + start, 8), size)

        def own(way, k, sub, part):
            return self.at(k if way == 0 else -k, sub, part)

        def hop(way, k, sub, part, source):
            if k == 1:
                target, device = mine, self.beside(way, sub)
            else:
                target, device = sub, self.beside(way, mine)
            return self.remote(
                source, self.rbuf.at[slot(way, k - 1, target, part)],
                self.rssem.at[0, way, k - 1, sub, part], self.rssem.at[1, way, k - 1, target, part], device,
            )

        def arrived(way, k, index, part):
            here = self.rbuf.at[slot(way, k, index, part)]
            return self.remote(
                here, here, self.rssem.at[0, way, k, index, part], self.rssem.at[1, way, k, index, part],
                self.beside(way, mine),
            )

        sent = []
        for k in (4, 3, 2, 1):
            for part in range(2):
                for sub in range(2):
                    for way in range(2):
                        first = 4 if sub == way else 3
                        if k > first:
                            continue
                        source = self.cbuf.at[own(way, k, sub, part)]
                        if k < first:
                            arrived(way, k, sub, part).wait_recv()
                            here = slot(way, k, sub, part)
                            self.rbuf[here, :] = self.rbuf[here, :] + self.cbuf[own(way, k, sub, part), :]
                            source = self.rbuf.at[here]
                        copy = hop(way, k, sub, part, source)
                        copy.start()
                        sent.append(copy)
            if k == 3:
                copy = self.remote(
                    self.cbuf.at[self.at(0, other)], self.fbuf.at[2], self.fsem.at[0], self.fsem.at[1], self.partner
                )
                copy.start()
        for part in range(2):
            for index in range(2):
                for way in range(2):
                    arrived(way, 0, index, part).wait_recv()
        arrivals = [self.rbuf[slot(0, 0, half), :] + self.rbuf[slot(1, 0, half), :] for half in (mine, other)]
        self.fbuf[0] = self.cbuf[self.at(0, mine), :] + arrivals[0]
        self.finish_pair(other)
        self.fbuf[1] = self.fbuf[2] + arrivals[1]
        for copy in sent:
            copy.wait_send()
        self.unpack(0, mine)
        self.unpack(1, other)

    def finish_pair(self, other):
        self.remote(
            self.cbuf.at[self.at(0, other)], self.fbuf.at[2], self.fsem.at[0], self.fsem.at[1], self.partner
        ).wait()

    def unpack(self, source, hh):
        third = self.lines // 3
        for c in range(2):
            start = c * self.lines
            self.unpacked[hh, c, 0 : self.lines, :] = self.fbuf[source, start : start + self.lines, 0:NG]
            for k in range(3):
                self.unpacked[hh, c, self.lines : self.half, k * 32 : (k + 1) * 32] = self.fbuf[
                    source, start + k * third : start + (k + 1) * third, NG:LP
                ]

    def correction(self, c):
        return jnp.concatenate([self.unpacked[0, c], self.unpacked[1, c]], 0)

    @staticmethod
    def scratch(nz, slots, rows):
        half = slots // 2
        lines = half * NG // LP
        block = 2 * lines
        dma = pltpu.SemaphoreType.DMA
        return [
            pltpu.VMEM((4 * rows * half, NG), F32),
            pltpu.VMEM((4 * rows, lines * LP), BF16),
            pltpu.VMEM((4 * rows, lines * LP), BF16),
            pltpu.VMEM((2, block, LP), F32),
            pltpu.VMEM((16 * block, LP), F32),
            pltpu.VMEM((2, 16, lines * LP), BF16),
            pltpu.VMEM((2, 16, lines * LP), BF16),
            pltpu.VMEM((2, 8, LP), F32),
            pltpu.VMEM((nz, 8, LP), F32),
            pltpu.VMEM((16 * block, LP), F32),
            pltpu.VMEM((16 * block, LP), F32),
            pltpu.VMEM((3, block, LP), F32),
            pltpu.VMEM((2, 2, half, NG), F32),
            dma((3, 2 * rows)), dma((2,)), dma((2, 2, 4, 2, 2)), dma((2,)), dma((nz,)), dma((nz,)), dma((2, 2, 4, 2, 2)), dma((2,)),
        ]


def kernel(nz, slots, planes, rows, *refs):
    inputs, resident, out_ref, rest = refs[:9], refs[9], refs[10], refs[11:]
    count = 30
    projector = Projector(nz, slots, rows, (resident,) + rest[count:])
    local_kernel(nz, slots, planes, inputs, out_ref, *rest[:count], projector=projector)


def on_device(wavefunctions, resident, potential, stick_column_table, kpoint, nz):
    slots = wavefunctions.shape[3]
    planes = potential.shape[0]
    rows = resident.shape[1]
    lanes = -(-2 * slots // LP) * LP
    consts = [jnp.asarray(t) for t in tables()]
    block = pltpu.VMEM((nz, planes, lanes), F32)
    dma = pltpu.SemaphoreType.DMA
    operands = (wavefunctions[0, 0], stick_column_table, potential, kpoint, *consts)
    out = pl.pallas_call(
        functools.partial(kernel, nz, slots, planes, rows),
        out_shape=jax.ShapeDtypeStruct((2, slots, NG), F32),
        in_specs=[pl.BlockSpec(memory_space=pl.ANY)] * 10,
        out_specs=pl.BlockSpec(memory_space=pltpu.VMEM),
        scratch_shapes=[pltpu.VMEM(x.shape, x.dtype) for x in operands]
        + [
            dma((9,)),
            block, block, block, block,
            pltpu.VMEM((2 * LP, nz * lanes), BF16),
            pltpu.VMEM((2 * LP, nz * lanes), BF16),
            pltpu.VMEM((2, planes * IXP, 2 * lanes), BF16),
            pltpu.VMEM((2, planes * IXP, 2 * lanes), BF16),
            pltpu.VMEM((IXP, nz * lanes), F32),
            pltpu.VMEM((planes * IXP, 2 * LP), F32),
            pltpu.VMEM((planes * IXP, 2 * LP), BF16),
            pltpu.VMEM((planes * IXP, 2 * LP), BF16),
            pltpu.VMEM((16, lanes), F32),
            pltpu.VMEM((planes * NG, LP), F32),
            pltpu.VMEM((LP, lanes), F32),
            pltpu.VMEM((slots, NG), F32),
            dma((nz,)), dma((nz,)), dma((nz,)), dma((nz,)),
        ]
        + Projector.scratch(nz, slots, rows),
        compiler_params=pltpu.CompilerParams(collective_id=0, has_side_effects=True),
    )(*operands, resident[0].reshape(2 * rows, slots, NG))
    return out[None, None]


def solution(mesh):
    in_specs = (
        P("kpt", "band", None, "plane", None),
        P("kpt", "band", None, "plane", None),
        P("plane", None),
        P("kpt", None),
        P("kpt", None),
    )
    out_specs = P("kpt", "band", None, "plane", None)
    return jax.shard_map(
        functools.partial(on_device, nz=mesh.shape["plane"]),
        mesh=mesh, in_specs=in_specs, out_specs=out_specs, check_vma=False,
    )
```

time: 101 us -> 92.7 us (0.918)
  Pallas kernels: 97.2 us -> 90.9 us
  local copies, waits for them, and re-layouts: 3.45 us -> 1.59 us
    pallas_call x1, Pallas kernels: 97.2 us -> 90.9 us  [on_device(): pl.pallas_call(functools.partial(kernel, nz, slots, planes, rows), out_sh...]
    reshape x1 -> x0, local copies, waits for them, and re-layouts: 1.85 us -> none  [on_device(): potential.reshape(planes, NG, NG)]
where the time goes in v2:
time: 92.7 us; the launch traced here: 92.5 us
  Pallas kernels  90.9 us (98%)
  local copies, waits for them, and re-layouts  1.59 us (2%)
    pallas_call x1, Pallas kernels, on_device(): pl.pallas_call(functools.partial(kernel, nz, slots, planes, rows), out_sh...  90.9 us

profile of v2, /device:TPU:1, one launch (start us, length us, event | category | flops | bytes accessed | tf_op | source)
XLA Modules:
  0.0 92.5 jit_solution(15640453610194445287)
XLA Ops:
  0.0 90.9 %shard_map.100 = f32[2,160,96]{2,1,0:T(8,128)} custom-call(f32[2,160,96]{2,1,0:T(8,128)} %bitcast.5, s32[1,1920]{1,0:T(1,128)} %refs_1_.1, f32[8,9216]{1,0:T(8,128)} %refs_2_.1, f32[1,3]{1,0:T(1,128)} %refs_3_.1, bf16[2,192,96]{2,1,0:T(8,128)(2,1)} %constant.10.clone.refs_4_, bf16[2,256,128]{2,1,0:T(8,128)(2,1)} %constant.11.clone.refs_5_, ...), custom_call_target="tpu_custom_call" | custom-call | tf_op jit(solution)/shard_map/pallas_call | solution.py:569
  91.0 1.6 %copy.12 = f32[1,1,2,160,96]{4,3,2,1,0:T(8,128)} copy(f32[1,1,2,160,96]{4,3,2,1,0:T(8,128)} %bitcast.4) | data formatting | bytes 245760

commit v3 on v2

--- a/solution.py
+++ b/solution.py
@@ -14,6 +14,11 @@
 HIGHEST = lax.Precision.HIGHEST
 MESH = pl.DeviceIdType.MESH
 RAD = NG // 4
+TAIL = 32
+SIZES = (32, 32, 16)
+STARTS = (0, 32, 64)
+LINES = (24, 24, 12)
+FIRSTS = (0, 24, 48)
 IXP = 64
 LP = 128
 F32 = jnp.float32
@@ -64,6 +69,13 @@
     return one(left[0], right[0]) + (one(left[1], right[0]) + one(left[0], right[1]))
 
 
+def pieces(slots):
+    for t, (size, start) in enumerate(zip(SIZES, STARTS)):
+        for c in range(2):
+            for h in range(2):
+                yield c, h, t * LP + (c * 2 + h) * size, size, h * (slots // 2) + start
+
+
 def local_kernel(
     nz, slots, planes,
     inputs, out_ref,
@@ -90,8 +102,9 @@
     from_imag = dot3(forward, split(wf_ref[1]), (1, 1))
     real = from_real[:NG] - from_imag[NG:]
     imag = from_imag[:NG] + from_real[NG:]
-    send1[:, :, 0:slots] = real.reshape(nz, planes, slots)
-    send1[:, :, slots : 2 * slots] = imag.reshape(nz, planes, slots)
+    for c, h, lane, size, slot in pieces(slots):
+        part = (real, imag)[c][:, slot : slot + size]
+        send1[:, :, lane : lane + size] = part.reshape(nz, planes, size)
     send1[:, :, 2 * slots :] = jnp.zeros((nz, planes, lanes - 2 * slots), F32)
     pl.semaphore_wait(barrier, nz - 1 + greeted)
 
@@ -116,9 +129,8 @@
     tabx[...] = jnp.full(tabx.shape, float(NG * NG), F32)
     columns = table_ref[...].astype(F32)
     for q in range(nz):
-        part = columns[:, q * slots : (q + 1) * slots]
-        tabx[q : q + 1, 0:slots] = part
-        tabx[q : q + 1, slots : 2 * slots] = part
+        for c, h, lane, size, slot in pieces(slots):
+            tabx[q : q + 1, lane : lane + size] = columns[:, q * slots + slot : q * slots + slot + size]
 
     def decode(column):
         ix = ((column + 0.5) * (1.0 / NG)).astype(jnp.int32).astype(F32)
@@ -128,7 +140,9 @@
     def block_lanes(q):
         return pl.ds(pl.multiple_of(q * lanes, LP), lanes)
 
-    second = lax.broadcasted_iota(jnp.int32, (1, lanes), 1) >= slots
+    lane = lax.broadcasted_iota(jnp.int32, (1, lanes), 1)
+    inner = jnp.where(lane < LP, lane, jnp.where(lane < 2 * LP, lane - LP, 2 * (lane - 2 * LP)))
+    second = inner >= LP // 2
     rows = lax.broadcasted_iota(jnp.int32, (2 * IXP, lanes), 0).astype(F32)
 
     @pl.loop(0, nz)
@@ -190,23 +204,34 @@
             at = slice((z + h) * IXP, (z + h + 1) * IXP)
             sph[at], spl[at] = high, low
 
-    out2 = []
-    for pair in reversed(range(nz // 2)):
-        offsets = ((nz - pair) % nz, pair + 1)
-        owners = [lax.rem(me + offset, nz) for offset in offsets]
-        phase = tuple(jnp.concatenate([b[:, block_lanes(q)] for q in owners], 1) for b in (bth, btl))
-        hot = jnp.concatenate([mask[:, block_lanes(q)] for q in owners], 1)
-        found = dot3((sph[...], spl[...]), phase, (1, 0))
-        picked = jnp.sum(found.reshape(planes, IXP, 2 * lanes) * hot[None], axis=1)
-        for place, (offset, q) in enumerate(zip(offsets, owners)):
-            part = picked[:, place * lanes : (place + 1) * lanes]
-            if offset == 0:
-                recv2[me] = part
-            else:
-                send2[q] = part
-                copy = transfer(send2, recv2, ssem2, rsem2, offset)
-                copy.start()
-                out2.append(copy)
+    def returning(t, offset):
+        there = lax.rem(me + offset, nz)
+        return pltpu.make_async_remote_copy(
+            src_ref=send2.at[t, there],
+            dst_ref=recv2.at[t, me],
+            send_sem=ssem2.at[t, offset],
+            recv_sem=rsem2.at[t, offset],
+            device_id={"plane": there},
+            device_id_type=MESH,
+        )
+
+    chunks = len(SIZES)
+    for t in range(chunks):
+        for pair in reversed(range(nz // 2)):
+            offsets = ((nz - pair) % nz, pair + 1)
+            owners = [lax.rem(me + offset, nz) for offset in offsets]
+            tiles = [pl.ds(pl.multiple_of(q * lanes + t * LP, LP), LP) for q in owners]
+            phase = tuple(jnp.concatenate([b[:, tile] for tile in tiles], 1) for b in (bth, btl))
+            hot = jnp.concatenate([mask[:, tile] for tile in tiles], 1)
+            found = dot3((sph[...], spl[...]), phase, (1, 0))
+            picked = jnp.sum(found.reshape(planes, IXP, 2 * LP) * hot[None], axis=1)
+            for place, (offset, q) in enumerate(zip(offsets, owners)):
+                part = picked[:, place * LP : (place + 1) * LP]
+                if offset == 0:
+                    recv2[t, me] = part
+                else:
+                    send2[t, q] = part
+                    returning(t, offset).start()
 
     column = tabx[pl.ds(me, 1), :]
     mx, my = decode(column)
@@ -221,24 +246,36 @@
     projector.flatten_resident()
     for copy in out1:
         copy.wait_send()
-    for copy in out2:
-        copy.wait()
-    trans[0:NG, :] = recv2[...].reshape(NG, lanes)
-    turned = trans[...].T
-    result = dot3(split(turned[: 2 * slots]), (zb[0], zb[1]), (1, 0))
-    alive = turned[:slots, NG + 1 : NG + 2]
-    kinetic = (KINETIC / (NG * NG)) * (turned[:slots, NG : NG + 1] + fz * fz) * alive
-    images = (
-        (result[:slots, :LP] + result[slots:, LP:])[:, :NG] + kinetic * wf_ref[0],
-        (result[slots:, :LP] - result[:slots, LP:])[:, :NG] + kinetic * wf_ref[1],
-    )
-    projector.pack(images)
-    for c in range(2):
-        out_ref[c] = images[c]
-    livecol[...] = jnp.broadcast_to(alive, livecol.shape)
-    first_gram = projector.gather()
-    projector.correct(projector.margin(first_gram))
-    projector.scatter()
+
+    def images_of(t):
+        for offset in range(1, nz):
+            returning(t, offset).wait_recv()
+        tile = slice(t * LP, (t + 1) * LP)
+        trans[0:NG, tile] = recv2[t].reshape(NG, LP)
+        turned = trans[:, tile].T
+        result = dot3(split(turned), (zb[0], zb[1]), (1, 0))
+        size, start = SIZES[t], STARTS[t]
+        upper, lower = result[: 2 * size], result[2 * size : 4 * size]
+        alive = turned[: 2 * size, NG + 1 : NG + 2]
+        kinetic = (KINETIC / (NG * NG)) * (turned[: 2 * size, NG : NG + 1] + fz * fz) * alive
+        spots = [slice(h * (slots // 2) + start, h * (slots // 2) + start + size) for h in range(2)]
+        own = [jnp.concatenate([wf_ref[c, spot] for spot in spots], 0) for c in range(2)]
+        images = (
+            (upper[:, :LP] + lower[:, LP:])[:, :NG] + kinetic * own[0],
+            (lower[:, :LP] - upper[:, LP:])[:, :NG] + kinetic * own[1],
+        )
+        wide = jnp.broadcast_to(alive, (2 * size, NG))
+        for h, spot in enumerate(spots):
+            for c in range(2):
+                out_ref[c, spot] = images[c][h * size : (h + 1) * size]
+            livecol[spot] = wide[h * size : (h + 1) * size]
+        projector.pack(images, t)
+
+    first_gram = projector.gather(images_of)
+    projector.scatter(projector.margin(first_gram))
+    for t in range(chunks):
+        for offset in range(1, nz):
+            returning(t, offset).wait_send()
     for c in range(2):
         out_ref[c] = out_ref[c] - livecol[...] * projector.correction(c)
 
@@ -254,7 +291,7 @@
         self.nz, self.half, self.rows = nz, slots // 2, rows
         self.lines = self.half * NG // LP
         self.block = 2 * self.lines
-        self.parts = ((0, 64), (64, self.block - 64))
+        self.parts = tuple((2 * first, 2 * count) for first, count in zip(FIRSTS, LINES))
         band = lax.axis_index("band")
         nb = 16
         self.me = lax.axis_index("plane")
@@ -304,21 +341,22 @@
             self.local_fetch(i).wait()
 
     def flatten_resident(self):
-        third = self.lines // 3
         span = 2 * self.half
-
-        @pl.loop(0, third)
-        def _(i):
-            for c in range(2):
-                for group in range(2 * self.rows // 16):
-                    base = group * 16 * span + c * self.half + i
-                    tail = self.dbuf[pl.ds(base + self.lines, 16, stride=span), :]
-                    for k in range(3):
-                        head = self.dbuf[pl.ds(base + k * third, 16, stride=span), :]
-                        line = jnp.concatenate([head, tail[:, k * 32 : (k + 1) * 32]], 1)
-                        lanes = pl.ds(pl.multiple_of((k * third + i) * LP, LP), LP)
-                        at = slice(c * 2 * self.rows + group * 16, c * 2 * self.rows + group * 16 + 16)
-                        self.dh[at, lanes], self.dl[at, lanes] = split(line)
+        for t, (count, first, slot) in enumerate(zip(LINES, FIRSTS, STARTS)):
+            third = count // 3
+
+            @pl.loop(0, third)
+            def _(i):
+                for c in range(2):
+                    for group in range(2 * self.rows // 16):
+                        base = group * 16 * span + c * self.half + slot + i
+                        tail = self.dbuf[pl.ds(base + count, 16, stride=span), :]
+                        for k in range(3):
+                            head = self.dbuf[pl.ds(base + k * third, 16, stride=span), :]
+                            line = jnp.concatenate([head, tail[:, k * TAIL : (k + 1) * TAIL]], 1)
+                            lanes = pl.ds(pl.multiple_of((first + k * third + i) * LP, LP), LP)
+                            at = slice(c * 2 * self.rows + group * 16, c * 2 * self.rows + group * 16 + 16)
+                            self.dh[at, lanes], self.dl[at, lanes] = split(line)
 
     def at(self, rel, sub, part=None):
         place = (ORDER.index(rel % 8) * 2 + sub) * self.block
@@ -327,27 +365,36 @@
         start, size = self.parts[part]
         return pl.ds(pl.multiple_of(place + start, 8), size)
 
-    def pack(self, images):
-        third = self.lines // 3
+    def pack(self, images, t):
+        size, count = SIZES[t], LINES[t]
+        third = count // 3
         for hh in range(2):
             for c in range(2):
-                part = images[c][hh * self.half : (hh + 1) * self.half]
-                self.packed[hh, c * self.lines : (c + 1) * self.lines, 0:NG] = part[: self.lines, :NG]
+                part = images[c][hh * size : (hh + 1) * size]
+                base = self.parts[t][0] + c * count
+                self.packed[hh, base : base + count, 0:NG] = part[:count]
                 for k in range(3):
-                    start = c * self.lines + k * third
-                    self.packed[hh, start : start + third, NG:LP] = part[self.lines :, k * 32 : (k + 1) * 32]
-
-    def gather(self):
+                    self.packed[hh, base + k * third : base + (k + 1) * third, NG:LP] = part[
+                        count:, k * TAIL : (k + 1) * TAIL
+                    ]
+
+    def gather(self, images_of):
         mine, other = self.core, 1 - self.core
-        pair = self.remote(
-            self.packed.at[other], self.abuf.at[self.at(0, mine)], self.psem.at[0], self.psem.at[1], self.partner
-        )
         sign = (-1, 1)
 
+        def rows(part):
+            start, size = self.parts[part]
+            return pl.ds(start, size)
+
+        def pair(part):
+            return self.remote(
+                self.packed.at[other, rows(part)], self.abuf.at[self.at(0, mine, part)],
+                self.psem.at[0, part], self.psem.at[1, part], self.partner,
+            )
+
         def first(way, core, part):
-            start, size = self.parts[part]
             return self.remote(
-                self.packed.at[core, pl.ds(start, size)], self.abuf.at[self.at(sign[way], mine, part)],
+                self.packed.at[core, rows(part)], self.abuf.at[self.at(sign[way], mine, part)],
                 self.agsem.at[0, way, 0, core, part], self.agsem.at[1, way, 0, mine, part], self.beside(way, core),
             )
 
@@ -359,26 +406,31 @@
                 self.beside(way, mine),
             )
 
-        started = [first(way, core, part) for part in range(2) for core in range(2) for way in range(2)]
-        for copy in started:
-            copy.start()
-        pair.start()
-        self.abuf[self.at(0, mine), :] = self.packed[mine]
-        for step in (1, 2, 3):
-            if step == 3:
-                pair.wait()
-                self.flatten_images(0)
-            for part in range(2):
-                for sub in range(2):
+        started = []
+        for step, part in (
+            (0, 0), (0, 1), (1, 0), (0, 2), (1, 1), (2, 0), (1, 2), (2, 1), (3, 0), (2, 2), (3, 1), (3, 2)
+        ):
+            if step == 0:
+                images_of(part)
+                for core in range(2):
                     for way in range(2):
-                        if step == 3 and sub != way:
-                            continue
-                        hop(way, step - 1, sub, part).wait_recv()
-                        copy = hop(way, step, sub, part)
-                        copy.start()
-                        started.append(copy)
+                        started.append(first(way, core, part))
+                        started[-1].start()
+                pair(part).start()
+                self.abuf[self.at(0, mine, part), :] = self.packed[mine, rows(part)]
+                continue
+            for sub in range(2):
+                for way in range(2):
+                    if step == 3 and sub != way:
+                        continue
+                    hop(way, step - 1, sub, part).wait_recv()
+                    started.append(hop(way, step, sub, part))
+                    started[-1].start()
+        for part in range(len(self.parts)):
+            pair(part).wait()
+        self.flatten_images(0)
         first_gram = self.gram(0)
-        for part in range(2):
+        for part in range(len(self.parts)):
             for way in range(2):
                 hop(way, 2, 1 - way, part).wait_recv()
                 hop(way, 3, way, part).wait_recv()
@@ -387,17 +439,16 @@
         return first_gram
 
     def flatten_images(self, group):
-        @pl.loop(0, self.lines)
-        def _(r):
-            lanes = pl.ds(pl.multiple_of(r * LP, LP), LP)
-            value = jnp.concatenate(
-                [
-                    self.abuf[pl.ds(group * 8 * self.block + c * self.lines + r, 8, stride=self.block), :]
-                    for c in range(2)
-                ],
-                0,
-            )
-            self.ih[group, :, lanes], self.il[group, :, lanes] = split(value)
+        for (row, _), count, first in zip(self.parts, LINES, FIRSTS):
+
+            @pl.loop(0, count)
+            def _(r):
+                lanes = pl.ds(pl.multiple_of((first + r) * LP, LP), LP)
+                base = group * 8 * self.block + row + r
+                value = jnp.concatenate(
+                    [self.abuf[pl.ds(base + c * count, 8, stride=self.block), :] for c in range(2)], 0
+                )
+                self.ih[group, :, lanes], self.il[group, :, lanes] = split(value)
 
     def gram(self, group):
         count = 2 * self.rows
@@ -431,21 +482,22 @@
             [jnp.concatenate([real, -imag], 1), jnp.concatenate([imag, real], 1)], 0
         )
 
-    def correct(self, margin):
-        left = split(margin)
+    def correct(self, left, t):
         batch = 4
-
-        @pl.loop(0, self.lines // batch)
+        count, first, row = LINES[t], FIRSTS[t], self.parts[t][0]
+
+        @pl.loop(0, count // batch)
         def _(g):
-            lanes = pl.ds(pl.multiple_of(g * batch * LP, LP), batch * LP)
+            lanes = pl.ds(pl.multiple_of((first + g * batch) * LP, LP), batch * LP)
             value = dot3(left, (self.dh[:, lanes], self.dl[:, lanes]), (1, 0))
             for i in range(batch):
                 for c in range(2):
-                    self.cbuf[pl.ds(c * self.lines + g * batch + i, 16, stride=self.block), :] = value[
+                    self.cbuf[pl.ds(row + c * count + g * batch + i, 16, stride=self.block), :] = value[
                         c * 16 : (c + 1) * 16, i * LP : (i + 1) * LP
                     ]
 
-    def scatter(self):
+    def scatter(self, margin):
+        left = split(margin)
         mine, other = self.core, 1 - self.core
 
         def slot(way, k, sub, part=None):
@@ -474,53 +526,61 @@
             )
 
         sent = []
-        for k in (4, 3, 2, 1):
-            for part in range(2):
+
+        def send(way, k, sub, part, source):
+            sent.append(hop(way, k, sub, part, source))
+            sent[-1].start()
+
+        parts = range(len(self.parts))
+        for part in parts:
+            self.correct(left, part)
+            for sub in range(2):
+                for way in range(2):
+                    k = 4 if sub == way else 3
+                    send(way, k, sub, part, self.cbuf.at[own(way, k, sub, part)])
+        self.remote(
+            self.cbuf.at[self.at(0, other)], self.fbuf.at[2], self.fsem.at[0], self.fsem.at[1], self.partner
+        ).start()
+        for k in (3, 2, 1):
+            for part in parts:
                 for sub in range(2):
                     for way in range(2):
-                        first = 4 if sub == way else 3
-                        if k > first:
+                        if k == 3 and sub != way:
                             continue
-                        source = self.cbuf.at[own(way, k, sub, part)]
-                        if k < first:
-                            arrived(way, k, sub, part).wait_recv()
-                            here = slot(way, k, sub, part)
-                            self.rbuf[here, :] = self.rbuf[here, :] + self.cbuf[own(way, k, sub, part), :]
-                            source = self.rbuf.at[here]
-                        copy = hop(way, k, sub, part, source)
-                        copy.start()
-                        sent.append(copy)
-            if k == 3:
-                copy = self.remote(
-                    self.cbuf.at[self.at(0, other)], self.fbuf.at[2], self.fsem.at[0], self.fsem.at[1], self.partner
-                )
-                copy.start()
-        for part in range(2):
+                        arrived(way, k, sub, part).wait_recv()
+                        here = slot(way, k, sub, part)
+                        self.rbuf[here, :] = self.rbuf[here, :] + self.cbuf[own(way, k, sub, part), :]
+                        send(way, k, sub, part, self.rbuf.at[here])
+        self.finish_pair(other)
+        for part in parts:
+            rows = pl.ds(*self.parts[part])
             for index in range(2):
                 for way in range(2):
                     arrived(way, 0, index, part).wait_recv()
-        arrivals = [self.rbuf[slot(0, 0, half), :] + self.rbuf[slot(1, 0, half), :] for half in (mine, other)]
-        self.fbuf[0] = self.cbuf[self.at(0, mine), :] + arrivals[0]
-        self.finish_pair(other)
-        self.fbuf[1] = self.fbuf[2] + arrivals[1]
+            for index, half, base in (
+                (0, mine, self.cbuf[self.at(0, mine, part), :]), (1, other, self.fbuf[2, rows])
+            ):
+                self.fbuf[index, rows] = base + (
+                    self.rbuf[slot(0, 0, half, part), :] + self.rbuf[slot(1, 0, half, part), :]
+                )
+                self.unpack(index, half, part)
         for copy in sent:
             copy.wait_send()
-        self.unpack(0, mine)
-        self.unpack(1, other)
 
     def finish_pair(self, other):
         self.remote(
             self.cbuf.at[self.at(0, other)], self.fbuf.at[2], self.fsem.at[0], self.fsem.at[1], self.partner
         ).wait()
 
-    def unpack(self, source, hh):
-        third = self.lines // 3
+    def unpack(self, source, hh, t):
+        count, slot = LINES[t], STARTS[t]
+        third = count // 3
         for c in range(2):
-            start = c * self.lines
-            self.unpacked[hh, c, 0 : self.lines, :] = self.fbuf[source, start : start + self.lines, 0:NG]
+            base = self.parts[t][0] + c * count
+            self.unpacked[hh, c, slot : slot + count, :] = self.fbuf[source, base : base + count, 0:NG]
             for k in range(3):
-                self.unpacked[hh, c, self.lines : self.half, k * 32 : (k + 1) * 32] = self.fbuf[
-                    source, start + k * third : start + (k + 1) * third, NG:LP
+                self.unpacked[hh, c, slot + count : slot + count + third, k * TAIL : (k + 1) * TAIL] = self.fbuf[
+                    source, base + k * third : base + (k + 1) * third, NG:LP
                 ]
 
     def correction(self, c):
@@ -546,7 +606,7 @@
             pltpu.VMEM((16 * block, LP), F32),
             pltpu.VMEM((3, block, LP), F32),
             pltpu.VMEM((2, 2, half, NG), F32),
-            dma((3, 2 * rows)), dma((2,)), dma((2, 2, 4, 2, 2)), dma((2,)), dma((nz,)), dma((nz,)), dma((2, 2, 4, 2, 2)), dma((2,)),
+            dma((3, 2 * rows)), dma((2, 3)), dma((2, 2, 4, 2, 3)), dma((2,)), dma((nz,)), dma((nz,)), dma((2, 2, 4, 2, 3)), dma((2,)),
         ]
 
 
@@ -574,7 +634,9 @@
         scratch_shapes=[pltpu.VMEM(x.shape, x.dtype) for x in operands]
         + [
             dma((9,)),
-            block, block, block, block,
+            block, block,
+            pltpu.VMEM((3, nz, planes, LP), F32),
+            pltpu.VMEM((3, nz, planes, LP), F32),
             pltpu.VMEM((2 * LP, nz * lanes), BF16),
             pltpu.VMEM((2 * LP, nz * lanes), BF16),
             pltpu.VMEM((2, planes * IXP, 2 * lanes), BF16),
@@ -587,7 +649,7 @@
             pltpu.VMEM((planes * NG, LP), F32),
             pltpu.VMEM((LP, lanes), F32),
             pltpu.VMEM((slots, NG), F32),
-            dma((nz,)), dma((nz,)), dma((nz,)), dma((nz,)),
+            dma((nz,)), dma((nz,)), dma((3, nz)), dma((3, nz)),
         ]
         + Projector.scratch(nz, slots, rows),
         compiler_params=pltpu.CompilerParams(collective_id=0, has_side_effects=True),

time: 92.7 us -> 96.6 us (1.042)
  Pallas kernels: 90.9 us -> 94.8 us
    pallas_call x1, Pallas kernels: 90.9 us -> 94.8 us  [on_device(): pl.pallas_call(functools.partial(kernel, nz, slots, planes, rows), out_sh...]
where the time goes in v3:
time: 96.6 us; the launch traced here: 96.4 us
  Pallas kernels  94.8 us (98%)
  local copies, waits for them, and re-layouts  1.59 us (2%)
    pallas_call x1, Pallas kernels, on_device(): pl.pallas_call(functools.partial(kernel, nz, slots, planes, rows), out_sh...  94.8 us

profile of v3, /device:TPU:1, one launch (start us, length us, event | category | flops | bytes accessed | tf_op | source)
XLA Modules:
  0.0 96.4 jit_solution(15448936096907267533)
XLA Ops:
  0.0 94.8 %shard_map.100 = f32[2,160,96]{2,1,0:T(8,128)} custom-call(f32[2,160,96]{2,1,0:T(8,128)} %bitcast.5, s32[1,1920]{1,0:T(1,128)} %refs_1_.1, f32[8,9216]{1,0:T(8,128)} %refs_2_.1, f32[1,3]{1,0:T(1,128)} %refs_3_.1, bf16[2,192,96]{2,1,0:T(8,128)(2,1)} %constant.10.clone.refs_4_, bf16[2,256,128]{2,1,0:T(8,128)(2,1)} %constant.11.clone.refs_5_, ...), custom_call_target="tpu_custom_call" | custom-call | tf_op jit(solution)/shard_map/pallas_call | solution.py:629
  94.8 1.6 %copy.12 = f32[1,1,2,160,96]{4,3,2,1,0:T(8,128)} copy(f32[1,1,2,160,96]{4,3,2,1,0:T(8,128)} %bitcast.4) | data formatting | bytes 245760

commit v4 on v2

--- a/solution.py
+++ b/solution.py
@@ -46,7 +46,9 @@
     zb = np.zeros((LP, 2 * LP))
     zb[:NG, :NG] = np.cos(full)
     zb[:NG, LP : LP + NG] = np.sin(full)
-    return [np.stack(split_np(table)) for table in (tz, ty, xf, xb, zb)]
+    high, low = split_np(xb)
+    wide = np.concatenate([high, low, high], axis=1)
+    return [np.stack(split_np(table)) for table in (tz, ty, xf)] + [wide, np.stack(split_np(zb))]
 
 
 def split(value):
@@ -55,13 +57,22 @@
     return high, low
 
 
+def stack3(pair, axis, left):
+    high, low = pair
+    return jnp.concatenate([high, low, high] if left else [high, high, low], axis)
+
+
+def contract(left, right, axes):
+    dims = (((axes[0],), (axes[1],)), ((), ()))
+    return lax.dot_general(left, right, dims, preferred_element_type=F32)
+
+
 def dot3(left, right, axes):
-    dims = (((axes[0],), (axes[1],)), ((), ()))
-
-    def one(a, b):
-        return lax.dot_general(a, b, dims, preferred_element_type=F32)
-
-    return one(left[0], right[0]) + (one(left[1], right[0]) + one(left[0], right[1]))
+    if left[0].shape[axes[0]] % LP == 0:
+        return contract(stack3(left, axes[0], True), stack3(right, axes[1], False), axes)
+    return contract(left[0], right[0], axes) + (
+        contract(left[1], right[0], axes) + contract(left[0], right[1], axes)
+    )
 
 
 def local_kernel(
@@ -148,16 +159,24 @@
     for x in range(NG):
         weights[pl.ds(x, planes, stride=NG), 0:NG] = pot_ref[:, x * NG : (x + 1) * NG]
 
-    for pair in range(nz // 2):
-        offsets = ((nz - pair) % nz, pair + 1)
-        owners = [lax.rem(me + offset, nz) for offset in offsets]
-        side = pair % 2
-        for place, (offset, q) in enumerate(zip(offsets, owners)):
-            if offset == 0:
-                values = send1[me]
-            else:
-                out1[(nz - offset) - 1].wait_recv()
-                values = recv1[q]
+    recv1[me] = send1[me]
+    acc[...] = jnp.zeros(acc.shape, F32)
+    deep = planes * IXP // 2
+
+    def pair_of(pair):
+        return lax.rem(me + nz - pair, nz), lax.rem(me + pair + 1, nz)
+
+    @pl.loop(0, nz // 2)
+    def _(pair):
+        owners = pair_of(pair)
+
+        @pl.when(pair > 0)
+        def _():
+            transfer(send1, recv1, ssem1, rsem1, pair).wait_recv()
+
+        transfer(send1, recv1, ssem1, rsem1, nz - 1 - pair).wait_recv()
+        for place, q in enumerate(owners):
+            values = recv1[q]
             hot = mask[:, block_lanes(q)].astype(BF16)
             into = slice(place * lanes, (place + 1) * lanes)
             for z in range(planes):
@@ -165,48 +184,61 @@
                 for g in range(IXP // 16):
                     part = hot[g * 16 : (g + 1) * 16]
                     at = slice(z * IXP + g * 16, z * IXP + (g + 1) * 16)
-                    lhh[side, at, into] = part * high
-                    lhl[side, at, into] = part * low
+                    lhh[0, at, into] = part * high
+                    lhl[0, at, into] = part * low
         phase = tuple(jnp.concatenate([b[:, block_lanes(q)] for q in owners], 1) for b in (bth, btl))
-        term = dot3((lhh[side], lhl[side]), phase, (1, 1))
-        acc[...] = term if pair == 0 else acc[...] + term
+        for h in range(2):
+            at = slice(h * deep, (h + 1) * deep)
+            acc[at] = acc[at] + dot3((lhh[0, at], lhl[0, at]), phase, (1, 1))
 
     to_x = (xf[0], xf[1])
-    to_k = (xb[0], xb[1])
-    for z in range(0, planes, 2):
-        a = acc[z * IXP : (z + 1) * IXP]
-        b = acc[(z + 1) * IXP : (z + 2) * IXP]
-        joined = jnp.concatenate(
-            [jnp.concatenate([a[:, :LP], b[:, :LP]], 1), jnp.concatenate([a[:, LP:], b[:, LP:]], 1)], 0
-        )
-        field = dot3(to_x, split(joined), (1, 0))
-        weight = jnp.concatenate([weights[z * NG : (z + 1) * NG], weights[(z + 1) * NG : (z + 2) * NG]], 1)
-        product = field * jnp.concatenate([weight, weight], 0)
-        back = dot3(to_k, split(product), (1, 0))
-        for h in range(2):
-            high, low = split(
-                jnp.concatenate([back[:IXP, h * LP : (h + 1) * LP], back[IXP:, h * LP : (h + 1) * LP]], 1)
-            )
-            at = slice((z + h) * IXP, (z + h + 1) * IXP)
-            sph[at], spl[at] = high, low
-
-    out2 = []
-    for pair in reversed(range(nz // 2)):
-        offsets = ((nz - pair) % nz, pair + 1)
-        owners = [lax.rem(me + offset, nz) for offset in offsets]
+    to_k = xb[...]
+
+    @pl.loop(0, planes // 4)
+    def _(quad):
+        for z2 in range(0, 4, 2):
+            z = quad * 4 + z2
+            a = acc[pl.ds(pl.multiple_of(z * IXP, IXP), IXP)]
+            b = acc[pl.ds(pl.multiple_of((z + 1) * IXP, IXP), IXP)]
+            joined = jnp.concatenate(
+                [jnp.concatenate([a[:, :LP], b[:, :LP]], 1), jnp.concatenate([a[:, LP:], b[:, LP:]], 1)], 0
+            )
+            field = dot3(to_x, split(joined), (1, 0))
+            weight = jnp.concatenate(
+                [weights[pl.ds(pl.multiple_of((z + h) * NG, 8), NG)] for h in range(2)], 1
+            )
+            product = field * jnp.concatenate([weight, weight], 0)
+            back = contract(to_k, stack3(split(product), 0, False), (1, 0))
+            for h in range(2):
+                high, low = split(
+                    jnp.concatenate([back[:IXP, h * LP : (h + 1) * LP], back[IXP:, h * LP : (h + 1) * LP]], 1)
+                )
+                at = pl.ds(pl.multiple_of((z + h) * IXP, IXP), IXP)
+                sph[at], spl[at] = high, low
+
+    @pl.loop(0, nz // 2)
+    def _(turn):
+        pair = nz // 2 - 1 - turn
+        owners = pair_of(pair)
         phase = tuple(jnp.concatenate([b[:, block_lanes(q)] for q in owners], 1) for b in (bth, btl))
         hot = jnp.concatenate([mask[:, block_lanes(q)] for q in owners], 1)
-        found = dot3((sph[...], spl[...]), phase, (1, 0))
-        picked = jnp.sum(found.reshape(planes, IXP, 2 * lanes) * hot[None], axis=1)
-        for place, (offset, q) in enumerate(zip(offsets, owners)):
-            part = picked[:, place * lanes : (place + 1) * lanes]
-            if offset == 0:
-                recv2[me] = part
-            else:
-                send2[q] = part
-                copy = transfer(send2, recv2, ssem2, rsem2, offset)
-                copy.start()
-                out2.append(copy)
+        halves = []
+        for h in range(2):
+            at = slice(h * deep, (h + 1) * deep)
+            found = dot3((sph[at], spl[at]), phase, (1, 0))
+            halves.append(jnp.sum(found.reshape(planes // 2, IXP, 2 * lanes) * hot[None], axis=1))
+        picked = jnp.concatenate(halves, 0)
+        for place, q in enumerate(owners):
+            send2[q] = picked[:, place * lanes : (place + 1) * lanes]
+
+        @pl.when(pair > 0)
+        def _():
+            transfer(send2, recv2, ssem2, rsem2, nz - pair).start()
+
+        transfer(send2, recv2, ssem2, rsem2, pair + 1).start()
+
+    recv2[me] = send2[me]
+    out2 = [transfer(send2, recv2, ssem2, rsem2, step) for step in range(1, nz)]
 
     column = tabx[pl.ds(me, 1), :]
     mx, my = decode(column)
@@ -401,7 +433,11 @@
 
     def gram(self, group):
         count = 2 * self.rows
-        gram = dot3((self.ih[group], self.il[group]), (self.dh[...], self.dl[...]), (1, 1))
+        middle = self.lines // 2 * LP
+        gram = sum(
+            dot3((self.ih[group, :, k], self.il[group, :, k]), (self.dh[:, k], self.dl[:, k]), (1, 1))
+            for k in (slice(0, middle), slice(middle, 2 * middle))
+        )
         real = gram[:8, :count] + gram[8:, count:]
         imag = gram[8:, :count] - gram[:8, count:]
         return jnp.concatenate([real, imag], 1)
@@ -432,13 +468,17 @@
         )
 
     def correct(self, margin):
-        left = split(margin)
+        left = stack3(split(margin), 1, True)
         batch = 4
 
         @pl.loop(0, self.lines // batch)
         def _(g):
             lanes = pl.ds(pl.multiple_of(g * batch * LP, LP), batch * LP)
-            value = dot3(left, (self.dh[:, lanes], self.dl[:, lanes]), (1, 0))
+            right = stack3((self.dh[:, lanes], self.dl[:, lanes]), 0, False)
+            middle = batch // 2 * LP
+            value = jnp.concatenate(
+                [contract(left, right[:, :middle], (1, 0)), contract(left, right[:, middle:], (1, 0))], 1
+            )
             for i in range(batch):
                 for c in range(2):
                     self.cbuf[pl.ds(c * self.lines + g * batch + i, 16, stride=self.block), :] = value[

time: 92.7 us -> 87.3 us (0.942)
  Pallas kernels: 90.9 us -> 85.5 us
    pallas_call x1, Pallas kernels: 90.9 us -> 85.5 us  [on_device(): pl.pallas_call(functools.partial(kernel, nz, slots, planes, rows), out_sh...]
where the time goes in v4:
time: 87.3 us; the launch traced here: 87.1 us
  Pallas kernels  85.5 us (98%)
  local copies, waits for them, and re-layouts  1.59 us (2%)
    pallas_call x1, Pallas kernels, on_device(): pl.pallas_call(functools.partial(kernel, nz, slots, planes, rows), out_sh...  85.5 us

profile of v4, /device:TPU:1, one launch (start us, length us, event | category | flops | bytes accessed | tf_op | source)
XLA Modules:
  0.0 87.1 jit_solution(11377747198908644088)
XLA Ops:
  0.0 85.5 %shard_map.100 = f32[2,160,96]{2,1,0:T(8,128)} custom-call(f32[2,160,96]{2,1,0:T(8,128)} %bitcast.5, s32[1,1920]{1,0:T(1,128)} %refs_1_.1, f32[8,9216]{1,0:T(8,128)} %refs_2_.1, f32[1,3]{1,0:T(1,128)} %refs_3_.1, bf16[2,192,96]{2,1,0:T(8,128)(2,1)} %constant.10.clone.refs_4_, bf16[2,256,128]{2,1,0:T(8,128)(2,1)} %constant.11.clone.refs_5_, ...), custom_call_target="tpu_custom_call" | custom-call | tf_op jit(solution)/shard_map/pallas_call | solution.py:609
  85.5 1.6 %copy.12 = f32[1,1,2,160,96]{4,3,2,1,0:T(8,128)} copy(f32[1,1,2,160,96]{4,3,2,1,0:T(8,128)} %bitcast.4) | data formatting | bytes 245760
